TPU v7x, 32 devices: a whole 2x2x4 slice. The times are simulated.
32 devices in a mesh: rep: 8 (over z, y), zero: 4 (over x, core).
Axes of the slice: x: 2, y: 2, z: 4, core: 2. Of those that a mesh axis runs over, the one named last changes fastest.
Arguments:
- tokens: bfloat16 [12288, 1280], P(('rep', 'zero')), may hold values from -6 to 6
- cotangent: bfloat16 [12288, 1280], P(('rep', 'zero')), may hold values from -6 to 6
- weights: bfloat16 [1280, 6, 1280], P('zero')
- vectors: bfloat16 [5, 1280], P(None, 'zero')
- error: float32 [10240, 6, 1280], P(('rep', 'zero'))
- previous_right_factors: float32 [6, 1280, 32], P(None, None, 'zero'), may hold values from -6 to 6
- momentum: float32 [1280, 6, 1280], P('zero', None, 'rep')
- vec_momentum: float32 [5, 1280], P(None, 'zero')
- prompt_len: int32 [8], P('rep'), may hold values from 512 to 1024, as said below
Outputs:
- result: bfloat16 [12288, 1280], P(('rep', 'zero'))
- grad_tokens: float32 [12288, 1280], P(('rep', 'zero'))
- grad_weights: float32 [1280, 6, 1280], P('zero', None, 'rep')
- grad_vectors: float32 [5, 1280], P(None, 'zero')
- new_error: float32 [10240, 6, 1280], P(('rep', 'zero'))
- fresh_right_factors: float32 [6, 1280, 32], P(None, None, 'zero')
- new_momentum: float32 [1280, 6, 1280], P('zero', None, 'rep')
- new_vec_momentum: float32 [5, 1280], P(None, 'zero')
- update_weights: float32 [1280, 6, 1280], P('zero', None, 'rep')
- update_vectors: float32 [5, 1280], P(None, 'zero')
Inputs may be any that keep to these rules, and one draw needn't show every extreme that they name: `prompt_len`: valid prompt rows of a group; the other prompt rows of its 1024 are padding.
All inputs are finite; a program needn't handle non-finite values.
Results may differ from a plain program's by a relative error of at most 0.028.
Values may be sent and summed in bfloat16 or wider, within the bound.
No kernel may reach another device: no remote copies, remote signals or barrier semaphores. Data moves between devices by JAX's collectives and lax.ppermute only.
A program may use at most 320 MiB of HBM per device.

v0:
```python
import functools
import math

import jax
import jax.numpy as jnp
import numpy as np
from jax import lax
from jax.experimental import pallas as pl
from jax.experimental.pallas import tpu as pltpu
from jax.sharding import PartitionSpec as P


HEADS = 16
PROMPT = 1024
LANES = 128

EPS = 1e-06
MU = 0.9
LOG2E = 1.442695041
NEG = -1e30
f32 = jnp.float32
bf16 = jnp.bfloat16


def rms_scale(field):
    return lax.rsqrt(jnp.mean(field * field, axis=-1, keepdims=True) + EPS)


def norm_back(field, scale, gain_vec, grad_in):
    weighted = grad_in * gain_vec
    inner = jnp.mean(field * weighted, axis=-1, keepdims=True)
    return scale * weighted - field * (scale * scale * scale) * inner


def to_pair(x, count):
    return lax.ppermute(x, "zero", [(i, i ^ 1) for i in range(count)])


def to_chip(x, count, shift):
    return lax.ppermute(x, "zero", [(i, (i + 2 * shift) % count) for i in range(count)])


def to_rep(x, count, step):
    return lax.ppermute(x, "rep", [(i, i ^ step) for i in range(count)])


def tables(chip, core, chips, quarter):
    at = np.arange(2 * chips)
    sign = np.repeat([-1, -1, 1], 2 * chips)
    shift = np.concatenate([at // 2, -(at // 2), at % chips])
    sign[2 * chips : 4 * chips] = 1
    flip = np.concatenate([at % 2, at % 2, at // chips])
    sign, shift, flip = (np.append(a, 0).astype(np.int32) for a in (sign, shift, flip))
    found = lax.rem(sign * chip + shift + chips, jnp.int32(chips)) * 2 + (core ^ flip)
    return jnp.where(np.arange(6 * chips + 1) == 6 * chips, quarter, found).astype(jnp.int32)


def gather_zero(x, count):
    out = []
    for shift in range(count // 2):
        block = x if shift == 0 else to_chip(x, count, shift)
        out += [block, to_pair(block, count)]
    return out


def sum_zero(x, count):
    x = x + to_pair(x, count)
    return sum((to_chip(x, count, s) for s in range(1, count // 2)), x)


def gather_weights(w_mats, count, quarter, rep_count):
    own = w_mats.shape[1]
    start = (3, quarter * (own // 4), 0)
    piece = lax.dynamic_slice(w_mats, start, (3, own // 4, w_mats.shape[2]))
    first = jnp.stack([to_chip(piece, count, s) for s in range(1, count // 2)])
    second = to_rep(first, rep_count, 1)
    third = to_rep(first, rep_count, 2)
    fourth = to_rep(second, rep_count, 2)
    mine = w_mats[3:6]
    far = [first, second, third, fourth]
    return [w_mats, to_pair(mine, count)] + far + [to_pair(x, count) for x in far]


def exchange_zero(near, far, count):
    out = [near[0], to_pair(near[1], count)]
    for shift in range(1, count // 2):
        held = to_chip(far[shift - 1], count, shift)
        out += [held, to_pair(held[1], count)]
    return out


def scatter_sum_zero(mine, away, count):
    held = mine.astype(f32) + to_pair(away, count).astype(f32)
    terms = [held[0]]
    for shift in range(1, count // 2):
        terms.append(to_chip(held[shift].astype(mine.dtype), count, shift).astype(f32))
    return terms


def sum_rep(x, count, dtype=f32):
    step = 1
    while step < count:
        low = x.astype(dtype)
        x = low.astype(f32) + to_rep(low, count, step).astype(f32)
        step *= 2
    return x


def dot(a, b, dims):
    return lax.dot_general(a, b, (dims, ((), ())), preferred_element_type=f32)


NN = ((1,), (0,))
NT = ((1,), (1,))
TN = ((0,), (0,))
ANY = pl.BlockSpec(memory_space=pl.ANY)
VMEM_LIMIT = 60 * 1024 * 1024


def params(steps=1):
    return pltpu.CompilerParams(
        dimension_semantics=("arbitrary",) * steps, vmem_limit_bytes=VMEM_LIMIT
    )


def cost(flops, moved):
    return pl.CostEstimate(flops=int(flops), bytes_accessed=int(moved), transcendentals=0)


def project_body(index_ref, tok_a, tok_b, gain_ref, w_ref, scale_ref, *refs):
    normed_ref, qkv_ref, query_ref = refs[-3:]
    step = pl.program_id(0)
    tok = jnp.where(step == 0, tok_a[...], tok_b[...]).astype(f32)
    normed = (tok * rms_scale(tok) * gain_ref[...]).astype(bf16)
    normed_ref[0] = normed
    own = w_ref.shape[1]
    out = dot(w_ref[...].reshape(3 * own, -1), normed, NT)
    query = out[:own]
    query_ref[0] = query.astype(bf16)
    qkv_ref[0, :own] = (query * scale_ref[...]).astype(bf16)
    qkv_ref[0, own:] = out[own:].astype(bf16)


def project(maps, shift, tok_a, tok_b, gain, w_mats, query_scale, count, held):
    first = count + 2 * shift
    rows, width = tok_a.shape
    own = w_mats.shape[1]
    shapes = (
        jax.ShapeDtypeStruct((count, rows, width), bf16),
        jax.ShapeDtypeStruct((count, 3 * own, rows), bf16),
        jax.ShapeDtypeStruct((count, own, rows), bf16),
    )
    whole = lambda *shape: pl.BlockSpec(shape, lambda s, at: (0,) * len(shape))
    held = () if held is None else tuple(held)
    return pl.pallas_call(
        project_body,
        out_shape=shapes,
        grid_spec=pltpu.PrefetchScalarGridSpec(
            num_scalar_prefetch=1,
            grid=(2,),
            in_specs=[
                whole(rows, width),
                whole(rows, width),
                whole(1, width),
                whole(3, own, width),
                whole(own, 1),
            ]
            + [ANY] * len(held),
            out_specs=[
                pl.BlockSpec((1, rows, width), lambda s, at: (at[first + s], 0, 0)),
                pl.BlockSpec((1, 3 * own, rows), lambda s, at: (at[first + s], 0, 0)),
                pl.BlockSpec((1, own, rows), lambda s, at: (at[first + s], 0, 0)),
            ],
        ),
        input_output_aliases={6 + i: i for i in range(len(held))},
        compiler_params=params(),
        cost_estimate=cost(2 * 2 * rows * 3 * own * width, 3 * own * width * 2 + 8 * rows * width),
    )(maps, tok_a, tok_b, gain, w_mats, query_scale, *held)


def masked_chunks(raw, size, diagonal, valid):
    chunks = []
    for j in range(raw.shape[0] // size):
        part = raw[j * size : (j + 1) * size]
        allowed = None
        if (j + 1) * size > PROMPT // 2:
            at = j * size + lax.broadcasted_iota(jnp.int32, part.shape, 0)
            allowed = at < valid
        if j == diagonal:
            causal = lax.broadcasted_iota(jnp.int32, part.shape, 0) <= lax.broadcasted_iota(
                jnp.int32, part.shape, 1
            )
            allowed = causal if allowed is None else allowed & causal
        chunks.append((part, allowed))
    return chunks


def units_of(count, prompt_rows, rows):
    for b in range(count):
        yield b, slice(0, prompt_rows), (b + 1) * prompt_rows, b, False
        yield b, slice(prompt_rows, rows), count * prompt_rows, None, True


def attend_body(valid_ref, place_ref, q_ref, k_ref, v_ref, *refs):
    count, _, rows = q_ref.shape
    *outs, all_ref, lse_ref, keys, values = refs
    size = PROMPT // count
    valid = valid_ref[0]
    for j in range(count):
        keys[j * size : (j + 1) * size, :] = k_ref[j, :, :size].T
        values[:, j * size : (j + 1) * size] = v_ref[j, :, :size]
    for b, lanes, seen, diagonal, own_cont in units_of(count, size, rows):
        query = q_ref[b, :, lanes]
        chunks = masked_chunks(dot(keys[:seen], query, NN), size, diagonal, valid)
        if own_cont:
            raw = dot(k_ref[b, :, size:].T, query, NN)
            chunks += masked_chunks(raw, raw.shape[0], 0, raw.shape[0])
        chunks = [p if ok is None else jnp.where(ok, p, NEG) for p, ok in chunks]
        top = chunks[0].max(axis=0, keepdims=True)
        for part in chunks[1:]:
            top = jnp.maximum(top, part.max(axis=0, keepdims=True))
        chunks = [jnp.exp(part - top) for part in chunks]
        total = chunks[0].sum(axis=0, keepdims=True)
        for part in chunks[1:]:
            total = total + part.sum(axis=0, keepdims=True)
        attended = None
        for j, part in enumerate(chunks):
            v_part = values[:, j * size : (j + 1) * size] if j * size < seen else v_ref[b, :, size:]
            term = dot(v_part, part.astype(bf16), NN)
            attended = term if attended is None else attended + term
        all_ref[b, :, lanes] = (attended / total).astype(bf16)
        lse_ref[0, b : b + 1, lanes] = top + jnp.log(total)
    chips = count // 2
    for p in range(count):
        block = all_ref[place_ref[2 * count + (p % 2) * chips + p // 2]]
        if p < 2:
            outs[p][...] = block
        else:
            outs[p // 2 + 1][p % 2] = block


def attend(valid, places, qkv, heads, head_dim):
    count, three_own, rows = qkv.shape
    own = three_own // 3
    block = lambda kind: pl.BlockSpec(
        (count, head_dim, rows), lambda h, *_: (0, kind * heads + h, 0)
    )
    pairs = PROMPT * PROMPT // 2 + PROMPT * count * (rows - PROMPT // count)
    return pl.pallas_call(
        attend_body,
        out_shape=(
            *[jax.ShapeDtypeStruct((own, rows), bf16)] * 2,
            *[jax.ShapeDtypeStruct((2, own, rows), bf16)] * (count // 2 - 1),
            jax.ShapeDtypeStruct((count, own, rows), bf16),
            jax.ShapeDtypeStruct((heads, count, rows), f32),
        ),
        grid_spec=pltpu.PrefetchScalarGridSpec(
            num_scalar_prefetch=2,
            grid=(heads,),
            in_specs=[block(0), block(1), block(2)],
            out_specs=[pl.BlockSpec((head_dim, rows), lambda h, *_: (h, 0))] * 2
            + [pl.BlockSpec((2, head_dim, rows), lambda h, *_: (0, h, 0))] * (count // 2 - 1)
            + [
                pl.BlockSpec((count, head_dim, rows), lambda h, *_: (0, h, 0)),
                pl.BlockSpec((1, count, rows), lambda h, *_: (h, 0, 0)),
            ],
            scratch_shapes=[
                pltpu.VMEM((PROMPT, head_dim), bf16),
                pltpu.VMEM((head_dim, PROMPT), bf16),
            ],
        ),
        compiler_params=params(),
        cost_estimate=cost(4 * 256 * heads * pairs, qkv.size * 3),
    )(valid, places, qkv, qkv, qkv)


def attend_back_body(
    valid_ref, place_ref, q_ref, k_ref, v_ref, query_ref, att_ref, lse_ref, scale_ref, spread_ref, *refs
):
    count, head_dim, rows = q_ref.shape
    parts = refs[:count]
    grad_ref, sum_ref, left_ref, keys, values, grad_keys, grad_values, grad_att = refs[count:]
    size = PROMPT // count
    valid = valid_ref[0]
    for i in range(count):
        grad_att[place_ref[count + i]] = parts[i][...].reshape(head_dim, rows)
    for j in range(count):
        keys[j * size : (j + 1) * size, :] = k_ref[j, :, :size].T
        values[j * size : (j + 1) * size, :] = v_ref[j, :, :size].T
    grad_keys[...] = jnp.zeros_like(grad_keys)
    grad_values[...] = jnp.zeros_like(grad_values)
    scale_sum = jnp.zeros((head_dim, 1), f32)
    for b, lanes, seen, diagonal, own_cont in units_of(count, size, rows):
        query = q_ref[b, :, lanes]
        grad_out = grad_att[b, :, lanes]
        query_rows = query.T
        grad_rows = grad_out.T
        lse = lse_ref[0, b : b + 1, lanes]
        delta = jnp.sum(
            att_ref[b, :, lanes].astype(f32) * grad_out.astype(f32),
            axis=0,
            keepdims=True,
        )
        grad_query = jnp.zeros(query.shape, f32)

        def block(key_rows, value_rows, chunk_size, diag, limit):
            raw = dot(key_rows, query, NN)
            grad_probs = dot(value_rows, grad_out, NN)
            probs, scores = [], []
            for j, (part, ok) in enumerate(masked_chunks(raw, chunk_size, diag, limit)):
                prob = jnp.exp(part - lse)
                if ok is not None:
                    prob = jnp.where(ok, prob, 0.0)
                score = prob * (grad_probs[j * chunk_size : (j + 1) * chunk_size] - delta)
                probs.append(prob.astype(bf16))
                scores.append(score.astype(bf16))
            return probs, scores

        probs, scores = block(keys[:seen], values[:seen], size, diagonal, valid)
        for j in range(len(probs)):
            at = slice(j * size, (j + 1) * size)
            grad_values[at, :] += dot(probs[j], grad_rows, NN)
            grad_keys[at, :] += dot(scores[j], query_rows, NN)
            grad_query += dot(k_ref[j, :, :size], scores[j], NN)
        if own_cont:
            probs, scores = block(
                k_ref[b, :, size:].T, v_ref[b, :, size:].T, rows - size, 0, rows - size
            )
            grad_query += dot(k_ref[b, :, size:], scores[0], NN)
            grad_ref[1, b, :, size:] = dot(scores[0], query_rows, NN).T.astype(bf16)
            grad_ref[2, b, :, size:] = dot(probs[0], grad_rows, NN).T.astype(bf16)
        scale_sum += jnp.sum(
            grad_query * query_ref[b, :, lanes].astype(f32), axis=1, keepdims=True
        )
        grad_ref[0, b, :, lanes] = (grad_query * scale_ref[:, 0:1]).astype(bf16)
    for j in range(count):
        at = slice(j * size, (j + 1) * size)
        grad_ref[1, j, :, :size] = grad_keys[at, :].T.astype(bf16)
        grad_ref[2, j, :, :size] = grad_values[at, :].T.astype(bf16)
    sum_ref[...] = jnp.broadcast_to(scale_sum, sum_ref.shape)
    twice = spread_ref.shape[1] // 3
    for m in range(3):
        left = jnp.zeros((twice, head_dim), f32)
        for b in range(count):
            terms = spread_ref[b, m * twice : (m + 1) * twice]
            left += dot(terms, grad_ref[m, b], NT)
        left_ref[0, m, :, :head_dim] = left[: twice // 2] + left[twice // 2 :]


def attend_back(valid, places, qkv, query, att, lse, query_scale, terms, parts, heads, head_dim):
    count, three_own, rows = qkv.shape
    own = three_own // 3
    size = PROMPT // count
    block = lambda kind: pl.BlockSpec(
        (count, head_dim, rows), lambda h, *_: (0, kind * heads + h, 0)
    )
    pairs = PROMPT * PROMPT // 2 + PROMPT * count * (rows - size)
    return pl.pallas_call(
        attend_back_body,
        out_shape=(
            jax.ShapeDtypeStruct((3, count, own, rows), bf16),
            jax.ShapeDtypeStruct((own, LANES), f32),
            jax.ShapeDtypeStruct((heads, 3, terms.shape[1] // 6, LANES), f32),
        ),
        grid_spec=pltpu.PrefetchScalarGridSpec(
            num_scalar_prefetch=2,
            grid=(heads,),
            in_specs=[
                block(0),
                block(1),
                block(2),
                block(0),
                block(0),
                pl.BlockSpec((1, count, rows), lambda h, *_: (h, 0, 0)),
                pl.BlockSpec((head_dim, 1), lambda h, *_: (h, 0)),
                pl.BlockSpec(terms.shape, lambda h, *_: (0, 0, 0)),
            ]
            + [
                pl.BlockSpec((1, head_dim, rows), lambda h, *_: (0, h, 0))
                if part.ndim == 3
                else pl.BlockSpec((head_dim, rows), lambda h, *_: (h, 0))
                for part in parts
            ],
            out_specs=[
                pl.BlockSpec((3, count, head_dim, rows), lambda h, *_: (0, 0, h, 0)),
                pl.BlockSpec((head_dim, LANES), lambda h, *_: (h, 0)),
                pl.BlockSpec((1, 3, terms.shape[1] // 6, LANES), lambda h, *_: (h, 0, 0, 0)),
            ],
            scratch_shapes=[
                pltpu.VMEM((PROMPT, head_dim), bf16),
                pltpu.VMEM((PROMPT, head_dim), bf16),
                pltpu.VMEM((PROMPT, head_dim), f32),
                pltpu.VMEM((PROMPT, head_dim), f32),
                pltpu.VMEM((count, head_dim, rows), bf16),
            ],
        ),
        compiler_params=params(),
        cost_estimate=cost(10 * 256 * heads * pairs, qkv.size * 5),
    )(valid, places, qkv, qkv, qkv, query, att, lse, query_scale, terms, *parts)


def feed_body(place_ref, tok_ref, cot_ref, vec_ref, *refs):
    count = (place_ref.shape[0] - 1) // 3
    far = count // 2 - 1
    att_parts = refs[:count]
    w_own, w_pair, *w_far = refs[count : count + 10]
    outs = refs[count + 10 :]
    att_grad_outs, outs = outs[: far + 2], outs[far + 2 :]
    (
        result_out,
        hidden_grad_out,
        inputs_out,
        grads_out,
        sums_ref,
        w,
        att,
        hidden,
        weighted,
        inputs,
        grads,
        result,
        att_grad,
        att_sems,
        w_sems,
        out_sems,
    ) = outs
    rows, width = tok_ref.shape
    own = width // count
    quarter = own // 4
    tile = 2 * LANES
    tiles = width // tile

    def load(source, target, sem):
        one = pltpu.make_async_copy(source, target, sem)
        one.start()
        return one

    att_copies = [
        load(
            att_parts[i].at[0] if i > 1 and i % 2 == 0 else att_parts[i],
            att.at[place_ref[count + i]],
            att_sems.at[i],
        )
        for i in range(count)
    ]
    w_copies = []
    for m in range(3):
        group = []
        for flip in range(2):
            source = w_pair.at[m] if flip else w_own.at[3 + m]
            group.append(load(source, w.at[m, place_ref[count + flip]], w_sems.at[m, len(group)]))
            pieces = w_far[4 * flip : 4 * flip + 4]
            for s in range(far):
                at = place_ref[count + 2 * (s + 1) + flip]
                for i in range(4):
                    start = pl.multiple_of((place_ref[3 * count] ^ i) * quarter, quarter)
                    target = w.at[m, at, pl.ds(start, quarter), :]
                    group.append(load(pieces[i].at[s, m], target, w_sems.at[m, len(group)]))
        w_copies.append(group)
    stores = []

    def store(source, target):
        stores.append(load(source, target, out_sems.at[len(stores)]))

    def rows_of(ref, p):
        return ref.at[pl.ds(pl.multiple_of(place_ref[2 * count + p] * own, own), own), :]

    def store_grads(m):
        for p in range(count):
            store(rows_of(grads.at[m], p), grads_out.at[m, p])

    grad_f = cot_ref[...]
    grads[2] = grad_f.T
    store_grads(2)
    for one in att_copies:
        one.wait()
    attended = att[...].reshape(width, rows).T
    inputs[0] = attended
    store(inputs.at[0], inputs_out.at[0])

    def w_rows(m, j):
        return w.at[m].reshape(width, width)[pl.ds(pl.multiple_of(j * tile, tile), tile), :]

    def w_cols(m, j):
        return w.at[m].reshape(width, width)[:, pl.ds(pl.multiple_of(j * tile, tile), tile)]

    def lanes(j):
        return pl.ds(pl.multiple_of(j * tile, tile), tile)

    for one in w_copies[0]:
        one.wait()

    def first(j, square):
        part = tok_ref[:, lanes(j)].astype(f32) + dot(attended, w_rows(0, j), NT)
        hidden[:, lanes(j)] = part
        return square + jnp.sum(part * part, axis=-1, keepdims=True)

    square = lax.fori_loop(0, tiles, first, jnp.zeros((rows, 1), f32))
    scale = lax.rsqrt(square / width + EPS)
    normed = (hidden[...] * scale * vec_ref[1:2, :]).astype(bf16)
    inputs[1] = normed
    store(inputs.at[1], inputs_out.at[1])
    for m in (1, 2):
        for one in w_copies[m]:
            one.wait()

    def second(j, carry):
        upper = dot(normed, w_rows(1, j), NT) + vec_ref[2:3, lanes(j)]
        gate = 1.0 / (1.0 + jnp.exp(-upper))
        inputs[2, :, lanes(j)] = (upper * gate).astype(bf16)
        grad_act = dot(grad_f, w_cols(2, j), NN)
        grad_up = (grad_act * gate * (1.0 + upper * (1.0 - gate))).astype(bf16)
        result[:, lanes(j)] = grad_up
        sums_ref[1:2, lanes(j)] = jnp.sum(grad_up.astype(f32), axis=0, keepdims=True)
        sums_ref[2:3, lanes(j)] = jnp.sum(
            cot_ref[:, lanes(j)].astype(f32), axis=0, keepdims=True
        )
        return carry

    lax.fori_loop(0, tiles, second, 0)
    store(inputs.at[2], inputs_out.at[2])
    grad_up = result[...]
    grads[1] = grad_up.T
    store_grads(1)
    activ = inputs[2]

    def third(j, inner):
        part = hidden[:, lanes(j)]
        out = dot(activ, w_rows(2, j), NT) + vec_ref[3:4, lanes(j)]
        result[:, lanes(j)] = (part + out).astype(bf16)
        grad_normed = dot(grad_up, w_cols(1, j), NN)
        sums_ref[0:1, lanes(j)] = jnp.sum(grad_normed * part * scale, axis=0, keepdims=True)
        turn = grad_normed * vec_ref[1:2, lanes(j)]
        weighted[:, lanes(j)] = turn
        return inner + jnp.sum(part * turn, axis=-1, keepdims=True)

    inner = lax.fori_loop(0, tiles, third, jnp.zeros((rows, 1), f32)) / width
    store(result, result_out)
    back = cot_ref[...].astype(f32) + (
        scale * weighted[...] - hidden[...] * (scale * scale * scale) * inner
    )
    weighted[...] = back
    store(weighted, hidden_grad_out)
    branch = back.astype(bf16)

    def fourth(j, carry):
        att_grad[lanes(j), :] = dot(branch, w_cols(0, j), NN).astype(bf16).T
        return carry

    lax.fori_loop(0, tiles, fourth, 0)
    for p in range(count):
        target = att_grad_outs[p] if p < 2 else att_grad_outs[p // 2 + 1].at[p % 2]
        store(rows_of(att_grad, (p % 2) * (far + 1) + p // 2), target)
    grads[0] = branch.T
    store_grads(0)
    for one in stores:
        one.wait()


def feed(places, tokens, cotangent, vec, att_parts, w_parts):
    count = len(att_parts)
    rows, width = tokens.shape
    own = width // count
    whole = lambda *shape: pl.BlockSpec(shape, lambda i, at: (0,) * len(shape))
    return pl.pallas_call(
        feed_body,
        out_shape=(
            *[jax.ShapeDtypeStruct((own, rows), bf16)] * 2,
            *[jax.ShapeDtypeStruct((2, own, rows), bf16)] * (count // 2 - 1),
            jax.ShapeDtypeStruct((rows, width), bf16),
            jax.ShapeDtypeStruct((rows, width), f32),
            jax.ShapeDtypeStruct((3, rows, width), bf16),
            jax.ShapeDtypeStruct((3, count, own, rows), bf16),
            jax.ShapeDtypeStruct((8, width), f32),
        ),
        grid_spec=pltpu.PrefetchScalarGridSpec(
            num_scalar_prefetch=1,
            grid=(1,),
            in_specs=[whole(rows, width), whole(rows, width), whole(*vec.shape)]
            + [ANY] * (count + len(w_parts)),
            out_specs=[ANY] * (5 + count // 2) + [whole(8, width)],
            scratch_shapes=[
                pltpu.VMEM((3, count, own, width), bf16),
                pltpu.VMEM((count, own, rows), bf16),
                pltpu.VMEM((rows, width), f32),
                pltpu.VMEM((rows, width), f32),
                pltpu.VMEM((3, rows, width), bf16),
                pltpu.VMEM((3, width, rows), bf16),
                pltpu.VMEM((rows, width), bf16),
                pltpu.VMEM((width, rows), bf16),
                pltpu.SemaphoreType.DMA((count,)),
                pltpu.SemaphoreType.DMA((3, 2 + 8 * (count // 2 - 1))),
                pltpu.SemaphoreType.DMA((5 + 4 * count,)),
            ],
        ),
        compiler_params=params(),
        cost_estimate=cost(12 * rows * width * width, 3 * width * width * 2 + rows * width * 24),
    )(places, tokens, cotangent, vec, *att_parts, *w_parts)


def split(x):
    high = x.astype(bf16)
    return jnp.concatenate([high, (x - high.astype(f32)).astype(bf16)], axis=-2)


def fold(x, rank):
    return x[..., :rank, :] + x[..., rank:, :]


def outer_body(grad_ref, input_ref, right_ref, *refs):
    *outs, left_mine_ref, left_away_ref = refs
    count, own, rows = grad_ref.shape[1:]
    chips = count // 2
    twice = right_ref.shape[1]
    grads = grad_ref[0]
    out = dot(grads.reshape(count * own, rows), input_ref[0], NN).astype(bf16)
    for b in range(count):
        outs[b][0] = out[b * own : (b + 1) * own]
    spread = dot(right_ref[...].reshape(count * twice, -1), input_ref[0], NT)
    for b in range(count):
        terms = split(fold(spread[b * twice : (b + 1) * twice], twice // 2))
        left = fold(dot(terms, grads[b], NT), twice // 2)
        if b < chips:
            left_mine_ref[b, 0] = left
        else:
            left_away_ref[b - chips, 0] = left


def outer(grads, inputs, rights):
    mats, count, own, rows = grads.shape
    width = count * own
    twice = rights.shape[1] // mats
    chips = count // 2
    left = jax.ShapeDtypeStruct((chips, mats, twice // 2, own), f32)
    part = jax.ShapeDtypeStruct((mats, own, width), bf16)
    part_spec = pl.BlockSpec((1, own, width), lambda m: (m, 0, 0))
    left_spec = pl.BlockSpec((chips, 1, twice // 2, own), lambda m: (0, m, 0, 0))
    return pl.pallas_call(
        outer_body,
        out_shape=(*[part] * count, left, left),
        grid=(mats,),
        in_specs=[
            pl.BlockSpec((1, count, own, rows), lambda m: (m, 0, 0, 0)),
            pl.BlockSpec((1, rows, width), lambda m: (m, 0, 0)),
            pl.BlockSpec((count, twice, width), lambda m: (0, m, 0)),
        ],
        out_specs=[part_spec] * count + [left_spec] * 2,
        compiler_params=params(),
        cost_estimate=cost(2 * mats * width * width * rows, mats * width * (width + rows) * 4),
    )(grads, inputs, rights)


def spread_body(normed_ref, right_ref, out_ref):
    mats_twice = right_ref.shape[0]
    twice = mats_twice // 3
    out = dot(right_ref[...], normed_ref[0], NT)
    for m in range(3):
        at = slice(m * twice, (m + 1) * twice)
        out_ref[0, at] = split(fold(out[at], twice // 2))


def spread(normed, rights):
    count, rows, width = normed.shape
    size = rights.shape[0]
    return pl.pallas_call(
        spread_body,
        out_shape=jax.ShapeDtypeStruct((count, size, rows), bf16),
        grid=(count,),
        in_specs=[
            pl.BlockSpec((1, rows, width), lambda b: (b, 0, 0)),
            pl.BlockSpec((size, width), lambda b: (0, 0)),
        ],
        out_specs=pl.BlockSpec((1, size, rows), lambda b: (b, 0, 0)),
        compiler_params=params(),
        cost_estimate=cost(2 * count * rows * width * size, normed.size * 2),
    )(normed, rights)


def error_left_body(error_ref, right_ref, out_ref):
    rank = right_ref.shape[1]
    error = error_ref[0]
    high = error.astype(bf16)
    low = (error - high.astype(f32)).astype(bf16)
    rights = split(right_ref[0])
    out = dot(high, rights, NT) + dot(low, rights, NT)
    out_ref[0] = fold(out.T, rank)


def error_left(error, right):
    mats, own, width = error.shape
    rank = right.shape[1]
    return pl.pallas_call(
        error_left_body,
        out_shape=jax.ShapeDtypeStruct((mats, rank, own), f32),
        grid=(mats,),
        in_specs=[
            pl.BlockSpec((1, own, width), lambda m: (m, 0, 0)),
            pl.BlockSpec((1, rank, width), lambda m: (m, 0, 0)),
        ],
        out_specs=pl.BlockSpec((1, rank, own), lambda m: (m, 0, 0)),
        compiler_params=params(),
        cost_estimate=cost(4 * error.size * rank, error.size * 4),
    )(error, right)


def input_back_body(order_ref, grad_ref, w_ref, *refs):
    count = len(refs) - 2
    tok_refs = refs[:count]
    out_ref, sum_ref = refs[count:]
    step = pl.program_id(0)
    own, rows = grad_ref.shape[2:]
    grads = grad_ref[...].reshape(3 * own, rows)
    part = dot(grads, w_ref[...].reshape(3 * own, -1), TN)
    out_ref[0] = part.astype(bf16)
    tok = tok_refs[0][...]
    for i in range(1, count):
        tok = jnp.where(step == i, tok_refs[i][...], tok)
    tok = tok.astype(f32)
    total = jnp.sum(part * (tok * rms_scale(tok)), axis=0, keepdims=True)

    @pl.when(step == 0)
    def _():
        sum_ref[...] = jnp.zeros_like(sum_ref)

    sum_ref[...] += jnp.broadcast_to(total, sum_ref.shape)


def input_back(maps, flip, grads, w_mats, toks):
    _, total, own, rows = grads.shape
    count = total // 2
    first = 2 * total + flip * count
    width = w_mats.shape[-1]
    return pl.pallas_call(
        input_back_body,
        out_shape=(
            jax.ShapeDtypeStruct((count, rows, width), bf16),
            jax.ShapeDtypeStruct((8, width), f32),
        ),
        grid_spec=pltpu.PrefetchScalarGridSpec(
            num_scalar_prefetch=1,
            grid=(count,),
            in_specs=[
                pl.BlockSpec((3, 1, own, rows), lambda s, at: (0, at[first + s], 0, 0)),
                pl.BlockSpec((3, own, width), lambda s, at: (0, 0, 0)),
            ]
            + [pl.BlockSpec((rows, width), lambda s, at: (0, 0))] * count,
            out_specs=[
                pl.BlockSpec((1, rows, width), lambda s, at: (s, 0, 0)),
                pl.BlockSpec((8, width), lambda s, at: (0, 0)),
            ],
        ),
        compiler_params=params(),
        cost_estimate=cost(2 * grads.size * width, grads.size * 2 + count * rows * width * 4),
    )(maps, grads, w_mats, *toks)


def right_body(ortho_ref, *refs):
    *terms, out = refs
    merged = sum(term[0].astype(f32) for term in terms)
    rank = ortho_ref.shape[1]
    out[0] = fold(dot(split(ortho_ref[0]), merged.astype(bf16), NN), rank).astype(bf16)


def tile_specs(rows, tile, first):
    return (
        pl.BlockSpec((1, rows, tile), lambda m, j: (first + m, 0, j)),
        pl.BlockSpec((1, rows, tile), lambda m, j: (m, 0, j)),
    )


def right_factors(ortho, error, first, terms):
    mats, own, width = terms[0].shape
    rank = ortho.shape[1]
    tile = width
    error_spec, term_spec = tile_specs(own, tile, first)
    return pl.pallas_call(
        right_body,
        out_shape=jax.ShapeDtypeStruct((mats, rank, width), bf16),
        grid=(mats, width // tile),
        in_specs=[pl.BlockSpec((1, rank, own), lambda m, j: (first + m, 0, 0)), error_spec]
        + [term_spec] * len(terms),
        out_specs=tile_specs(rank, tile, first)[1],
        compiler_params=params(2),
        cost_estimate=cost(4 * mats * own * width * rank, mats * own * width * 6),
    )(ortho, error, *terms)


def triple(x, pattern):
    high = x.astype(bf16)
    low = (x - high.astype(f32)).astype(bf16)
    return jnp.concatenate([low if p else high for p in pattern], axis=0)


def finish_body(rate, count, ortho_ref, right_ref, slice_ref, mom_ref, *refs):
    terms = refs[:count]
    err_ref, fresh_ref, grad_ref, new_ref, upd_ref = refs[-5:]
    ortho = triple(ortho_ref[0], (0, 0, 1))
    fresh_ref[0] = right_ref[0]
    approx = dot(ortho, triple(right_ref[0], (0, 1, 0)), TN)
    err_ref[0] = sum(term[0].astype(f32) for term in terms) - approx

    @pl.when(pl.program_id(1) == 0)
    def _():
        grad = dot(triple(slice_ref[0], (0, 1, 0)), ortho, TN)
        grad_ref[0] = grad
        new = MU * mom_ref[0] + grad
        new_ref[0] = new
        upd_ref[0] = -rate * new


def finish(rate, ortho, right, right_slice, momentum, error, first, terms, held):
    half, own, width = terms[0].shape
    mats, rank = ortho.shape[:2]
    cut = momentum.shape[1]
    tile = width
    error_spec, term_spec = tile_specs(own, tile, first)
    fresh_spec, right_spec = tile_specs(rank, tile, first)
    per = lambda *shape: pl.BlockSpec((1,) + shape, lambda m, j: (m, 0, 0))
    at = lambda *shape: pl.BlockSpec((1,) + shape, lambda m, j: (first + m, 0, 0))
    shape = jax.ShapeDtypeStruct(momentum.shape, f32)
    held = () if held is None else tuple(held)
    return pl.pallas_call(
        functools.partial(finish_body, rate, 1 + len(terms)),
        out_shape=(
            jax.ShapeDtypeStruct((mats, own, width), f32),
            jax.ShapeDtypeStruct((mats, rank, width), f32),
            shape,
            shape,
            shape,
        ),
        grid=(half, width // tile),
        in_specs=[at(rank, own), right_spec, per(rank, cut), at(cut, own), error_spec]
        + [term_spec] * len(terms)
        + [ANY] * len(held),
        out_specs=[error_spec, fresh_spec] + [at(cut, own)] * 3,
        input_output_aliases={5 + len(terms) + i: i for i in range(len(held))},
        compiler_params=params(2),
        cost_estimate=cost(half * own * width * 48, half * own * width * 10),
    )(ortho, right, right_slice, momentum, error, *terms, *held)


def close_rows_body(tok_ref, gain_ref, hidden_ref, mine_ref, paired_ref, *refs):
    *far, out = refs
    grad = mine_ref[0].astype(f32) + paired_ref[0].astype(f32)
    for term in far:
        grad += term[...].astype(f32)
    tok = tok_ref[...].astype(f32)
    out[...] = hidden_ref[...] + norm_back(tok, rms_scale(tok), gain_ref[...], grad)


def close_rows(tokens, gain, grad_hidden, mine, paired, far):
    rows, width = tokens.shape
    row = pl.BlockSpec((LANES, width), lambda i: (i, 0))
    first = pl.BlockSpec((1, LANES, width), lambda i: (0, i, 0))
    return pl.pallas_call(
        close_rows_body,
        out_shape=jax.ShapeDtypeStruct((rows, width), f32),
        grid=(rows // LANES,),
        in_specs=[row, pl.BlockSpec((1, width), lambda i: (0, 0)), row, first, first]
        + [row] * len(far),
        out_specs=row,
        compiler_params=params(),
        cost_estimate=cost(20 * rows * width, 18 * rows * width),
    )(tokens, gain, grad_hidden, mine, paired, *far)


def ortho_body(left_ref, out_ref):
    rank = left_ref.shape[0]
    columns = [left_ref[c] for c in range(rank)]
    for e in range(rank):
        done = columns[e]
        done = done * lax.rsqrt(jnp.sum(done * done, axis=-1, keepdims=True) + EPS)
        out_ref[:, e, :] = done
        for c in range(e + 1, rank):
            columns[c] = columns[c] - jnp.sum(done * columns[c], axis=-1, keepdims=True) * done


def orthonormal(left):
    rank, mats, own = left.shape
    return pl.pallas_call(
        ortho_body, out_shape=jax.ShapeDtypeStruct((mats, rank, own), f32)
    )(left)


def on_device(
    tokens,
    cotangent,
    weights,
    vectors,
    error,
    previous_right_factors,
    momentum,
    vec_momentum,
    prompt_len,
):
    zero_index = lax.axis_index("zero")
    rep_index = lax.axis_index("rep")
    n = lax.axis_size("zero")
    chips = n // 2
    rep_count = lax.axis_size("rep")
    rows, width = tokens.shape
    head_dim = width // HEADS
    heads = HEADS // n
    own = weights.shape[0]
    group_rows = n * rows
    quarter = rep_index & 3
    maps = tables(zero_index >> 1, zero_index & 1, chips, quarter)
    w_mats = weights.transpose(1, 0, 2)
    old_right = previous_right_factors.transpose(0, 2, 1)
    rank = old_right.shape[1]
    error_mats = error.transpose(1, 0, 2)

    column = zero_index * own
    spaced = lax.dynamic_update_slice(jnp.zeros((5, width), bf16), vectors, (0, column))
    spaced = sum((to_chip(spaced, n, s) for s in range(1, chips)), spaced)
    vec_float = (spaced + to_pair(spaced, n)).astype(f32)
    tok_parts = gather_zero(tokens, n)
    pairs_right = split(old_right)
    right_parts = gather_zero(pairs_right[3:6].reshape(6 * rank, width), n)
    flipped = [2 * ((chips - s) % chips) + f for f in range(2) for s in range(chips)]
    far_rights = jnp.stack([right_parts[i] for i in flipped])
    error_part = error_left(error_mats, old_right)
    far_parts = gather_weights(w_mats, n, quarter, rep_count)

    scale_raw = vectors[4].astype(f32)
    scale_const = LOG2E / math.sqrt(head_dim)
    query_scale = (scale_const * jax.nn.softplus(scale_raw)).reshape(own, 1)
    held = None
    for s in range(chips):
        held = project(
            maps,
            s,
            tok_parts[2 * s],
            tok_parts[2 * s + 1],
            vec_float[0:1],
            w_mats,
            query_scale,
            n,
            held,
        )
    normed_all, qkv, query = held
    *att_blocks, att_all, lse = attend(prompt_len, maps, qkv, heads, head_dim)
    att_parts = exchange_zero(att_blocks[:2], att_blocks[2:], n)
    terms = spread(normed_all, pairs_right[0:3].reshape(6 * rank, width))
    *att_grads, result, grad_hidden, far_inputs, far_grads, sums = feed(
        maps, tokens, cotangent, vec_float, att_parts, far_parts
    )
    grad_parts = exchange_zero(att_grads[:2], att_grads[2:], n)
    *blocks, left_mine, left_away = outer(far_grads, far_inputs, far_rights)
    far_sums = []
    for s in range(1, chips):
        paired = to_pair(blocks[chips + s], n)
        far_sums.append((blocks[s].astype(f32) + paired.astype(f32)).astype(bf16))
    left_far = sum(scatter_sum_zero(left_mine, left_away, n))
    grad_parts, far_sums = lax.optimization_barrier((grad_parts, far_sums))
    far_terms = [to_chip(far_sums[s - 1], n, s) for s in range(1, chips)]
    grads, scale_sums, left_heads = attend_back(
        prompt_len,
        maps,
        qkv,
        query,
        att_all,
        lse,
        query_scale,
        terms,
        grad_parts,
        heads,
        head_dim,
    )
    left_near = left_heads[..., :head_dim].transpose(1, 2, 0, 3).reshape(3, rank, own)
    left = jnp.concatenate([left_near, left_far], axis=0) + error_part
    left = sum_rep(left.transpose(1, 0, 2), rep_count) / rep_count
    ortho = orthonormal(left)

    toks = [tok_parts[i] for i in flipped]
    n1_away, gain_away = input_back(maps, 1, grads, w_mats, toks[chips:])
    n1_mine, gain_mine = input_back(maps, 0, grads, w_mats, toks[:chips])
    near = jnp.einsum("mbot,bti->moi", grads, normed_all, preferred_element_type=f32)
    n1_paired = to_pair(n1_away, n)
    n1_far = []
    for s in range(1, chips):
        sent = (n1_mine[s].astype(f32) + n1_paired[s].astype(f32)).astype(bf16)
        n1_far.append(to_chip(sent, n, s))
    grad_tokens = close_rows(tokens, vec_float[0:1], grad_hidden, n1_mine, n1_paired, n1_far)

    near_terms = [near]
    far_terms = [blocks[0], to_pair(blocks[chips], n), *far_terms]
    rep_width = width // rep_count
    cut_at = rep_index * rep_width
    step_rate = 0.03 / math.sqrt(group_rows)
    momentum_mats = momentum.transpose(1, 2, 0)

    def close(right, cut_at, first, parts, held):
        own_right = lax.dynamic_slice_in_dim(right, cut_at, rep_width, 1)
        right, own_right = (x[: 3 * rank].reshape(3, rank, -1) for x in (right, own_right))
        return finish(
            step_rate, ortho, right, own_right, momentum_mats, error_mats, first, parts, held
        )

    right = right_factors(ortho, error_mats, 0, near_terms).reshape(3 * rank, width)
    right = sum_rep(right, rep_count, bf16) / rep_count
    held = close(right, cut_at, 0, near_terms, None)

    vec_sums = jnp.concatenate([gain_away[0:1] + gain_mine[0:1], sums[0:3]], axis=0)
    vec_sums = lax.dynamic_slice_in_dim(sum_zero(vec_sums, n), column, own, 1)
    grad_scale_raw = scale_sums[:, 0] * scale_const * jax.nn.sigmoid(scale_raw)
    vec_sums = jnp.concatenate([vec_sums, grad_scale_raw[None]], axis=0)
    vec_rows = -(-vec_sums.size // width)
    vec_flat = jnp.pad(vec_sums.reshape(-1), (0, vec_rows * width - vec_sums.size))
    vec_flat = vec_flat.reshape(vec_rows, width).astype(bf16)
    right = right_factors(ortho, error_mats, 3, far_terms)
    packed = jnp.concatenate([right.reshape(3 * rank, width), vec_flat], axis=0)
    packed = sum_rep(packed, rep_count, bf16) / rep_count
    held = close(packed, lax.optimization_barrier(cut_at), 3, far_terms, held)
    new_error, fresh, *moved = held
    new_error = new_error.transpose(1, 0, 2)
    fresh_right_factors = fresh.transpose(0, 2, 1)
    grad_weights, new_momentum, update_weights = (x.transpose(2, 0, 1) for x in moved)
    grad_vectors = packed[3 * rank :].reshape(-1)[: vec_sums.size].reshape(vec_sums.shape)
    new_vec_momentum = MU * vec_momentum + grad_vectors
    update_vectors = -step_rate * new_vec_momentum
    return (
        result,
        grad_tokens,
        grad_weights,
        grad_vectors,
        new_error,
        fresh_right_factors,
        new_momentum,
        new_vec_momentum,
        update_weights,
        update_vectors,
    )


def solution(mesh):
    in_specs = (
        P(("rep", "zero"), None),
        P(("rep", "zero"), None),
        P("zero", None, None),
        P(None, "zero"),
        P(("rep", "zero"), None, None),
        P(None, None, "zero"),
        P("zero", None, "rep"),
        P(None, "zero"),
        P("rep"),
    )
    out_specs = (
        P(("rep", "zero"), None),
        P(("rep", "zero"), None),
        P("zero", None, "rep"),
        P(None, "zero"),
        P(("rep", "zero"), None, None),
        P(None, None, "zero"),
        P("zero", None, "rep"),
        P(None, "zero"),
        P("zero", None, "rep"),
        P(None, "zero"),
    )

    return jax.shard_map(
        on_device, mesh=mesh, in_specs=in_specs, out_specs=out_specs, check_vma=False
    )
```

profile of v0, /device:TPU:0, one launch (start us, length us, event | category | flops | bytes accessed | tf_op | source)
XLA Modules:
  0.0 304.6 jit_solution(2679382564917903329)
XLA Ops:
  1.2 2.6 collective-permute-start.2
  12.3 14.3 %collective-permute-done.2.tok_a.refs_1_ = bf16[384,1280]{1,0:T(8,128)(2,1)} collective-permute-done((bf16[384,1280]{1,0:T(8,128)(2,1)}, bf16[384,1280]{1,0:T(8,128)(2,1)}, u32[]{:S(2)}, u32[]{:S(2)}) %collective-permute-start.2) | collective-permute-done | bytes 983072 | tf_op jit(solution)/shard_map/ppermute | solution.py:40
  31.5 8.8 %collective-permute-done.9 = bf16[3,80,1280]{2,1,0:T(8,128)(2,1)} collective-permute-done((bf16[3,80,1280]{2,1,0:T(8,128)(2,1)}, bf16[3,80,1280]{2,1,0:T(8,128)(2,1)}, u32[]{:S(2)}, u32[]{:S(2)}) %collective-permute-start.9) | collective-permute-done | bytes 614432 | tf_op jit(solution)/shard_map/ppermute | solution.py:40
  43.5 7.4 %shard_map.204 = (bf16[4,384,1280]{2,1,0:T(8,128)(2,1)}, bf16[4,960,384]{2,1,0:T(8,128)(2,1)}, bf16[4,320,384]{2,1,0:T(8,128)(2,1)}) custom-call(s32[13]{0:T(128)} %fusion.13.index_ref.place_ref.order_ref, bf16[384,1280]{1,0:T(8,128)(2,1)} %tok_ref.3, bf16[384,1280]{1,0:T(8,128)(2,1)} %collective-permute-done.4.tok_b.refs_0_, f32[1,1280]{1,0:T(1,128)} %slice.86.gain_ref, ...), custom_call_target="tpu_custom_call" | custom-call | flops 1887436800 | bytes 6389760 | tf_op jit(solution)/shard_map/pallas_call | solution.py:155
  52.6 7.4 %shard_map.205 = (bf16[4,384,1280]{2,1,0:T(8,128)(2,1)}, bf16[4,960,384]{2,1,0:T(8,128)(2,1)}, bf16[4,320,384]{2,1,0:T(8,128)(2,1)}) custom-call(s32[13]{0:T(128)} %fusion.13.index_ref.place_ref.order_ref, bf16[384,1280]{1,0:T(8,128)(2,1)} %collective-permute-done.2.tok_a.refs_1_, ...), custom_call_target="tpu_custom_call", output_to_operand_aliasing={{0}: (6, {}), {1}: (7, {}), {2}: (8, {})} | custom-call | flops 1887436800 | bytes 6389760 | tf_op jit(solution)/shard_map/pallas_call | solution.py:155
  61.0 16.7 %shard_map.206 = (bf16[320,384]{1,0:T(8,128)(2,1)}, bf16[320,384]{1,0:T(8,128)(2,1)}, bf16[2,320,384]{2,1,0:T(8,128)(2,1)}, bf16[4,320,384]{2,1,0:T(8,128)(2,1)}, f32[4,4,384]{2,1,0:T(4,128)}) custom-call(s32[1]{0:T(128)S(6)} %copy.71.valid_ref, s32[13]{0:T(128)} %fusion.13.index_ref.place_ref.order_ref, ...), custom_call_target="tpu_custom_call" | custom-call | flops 4294967296 | bytes 4423680 | tf_op jit(solution)/shard_map/pallas_call | solution.py:249
  80.3 11.0 %collective-permute-done.6.refs_2_ = bf16[2,320,384]{2,1,0:T(8,128)(2,1)S(1)} collective-permute-done((bf16[2,320,384]{2,1,0:T(8,128)(2,1)}, bf16[2,320,384]{2,1,0:T(8,128)(2,1)S(1)}, u32[]{:S(2)}, u32[]{:S(2)}) %collective-permute-start.6) | collective-permute-done | bytes 491552 | tf_op jit(solution)/shard_map/ppermute | solution.py:40
  95.8 23.9 %shard_map.207 = (bf16[320,384]{1,0:T(8,128)(2,1)}, bf16[320,384]{1,0:T(8,128)(2,1)}, bf16[2,320,384]{2,1,0:T(8,128)(2,1)}, bf16[384,1280]{1,0:T(8,128)(2,1)}, f...) custom-call(s32[13]{0:T(128)} %fusion.13.index_ref.place_ref.order_ref, ...), custom_call_target="tpu_custom_call" | custom-call | flops 7549747200 | bytes 21626880 | tf_op jit(solution)/shard_map/pallas_call | solution.py:565
  119.7 10.5 %shard_map.209 = (bf16[3,320,1280]{2,1,0:T(8,128)(2,1)}, bf16[3,320,1280]{2,1,0:T(8,128)(2,1)}, bf16[3,320,1280]{2,1,0:T(8,128)(2,1)}, bf16[3,320,1280]{2,1,0:T(...) custom-call(bf16[3,4,320,384]{3,2,1,0:T(8,128)(2,1)} %get-tuple-element.73.grad_ref, ...), custom_call_target="tpu_custom_call" | custom-call | flops 3774873600 | bytes 25559040 | tf_op jit(solution)/shard_map/pallas_call | solution.py:638
  133.2 2.1 collective-permute-done.26
  137.8 7.7 %shard_map.214 = f32[6,8,320]{2,1,0:T(8,128)} custom-call(f32[6,320,1280]{2,1,0:T(8,128)} %bitcast.60, f32[6,8,1280]{2,1,0:T(8,128)} %bitcast.74), custom_call_target="tpu_custom_call" | custom-call | flops 78643200 | bytes 9830400 | tf_op jit(solution)/shard_map/pallas_call | solution.py:692
  145.5 4.6 %shard_map.208.spread_ref = bf16[4,48,384]{2,1,0:T(8,128)(2,1)} custom-call(bf16[4,384,1280]{2,1,0:T(8,128)(2,1)} %get-tuple-element.69.normed_ref, bf16[48,1280]{1,0:T(8,128)(2,1)} %bitcast.80), custom_call_target="tpu_custom_call" | custom-call | flops 188743680 | bytes 3932160 | tf_op jit(solution)/shard_map/pallas_call | solution.py:665
  150.9 4.4 %add_convert_fusion = bf16[3,320,1280]{2,1,0:T(8,128)(2,1)} fusion(bf16[3,320,1280]{2,1,0:T(8,128)(2,1)} %collective-permute-done.23, bf16[3,320,1280]{2,1,0:T(8,128)(2,1)} %get-tuple-element.75), kind=kLoop, calls=%fused_computation | loop fusion | flops 4915200 | bytes 7372800 | tf_op jit(solution)/shard_map/convert_element_type | solution.py:953
  156.3 21.0 %shard_map.210 = (bf16[3,4,320,384]{3,2,1,0:T(8,128)(2,1)}, f32[320,128]{1,0:T(8,128)}, f32[4,3,8,128]{3,2,1,0:T(8,128)}) custom-call(s32[1]{0:T(128)S(6)} %copy.71.valid_ref, s32[13]{0:T(128)} %fusion.13.index_ref.place_ref.order_ref, bf16[4,960,384]{2,1,0:T(8,128)(2,1)} %get-tuple-element.60.q_ref.k_ref.v_ref, ...), custom_call_target="tpu_custom_call" | custom-call | flops 10737418240 | bytes 7372800 | tf_op jit(solution)/shard_map/pallas_call | solution.py:358
  179.8 8.8 %convolution_bitcast_fusion.refs_1_ = f32[3,320,1280]{2,1,0:T(8,128)} fusion(bf16[3,4,320,384]{3,2,1,0:T(8,128)(2,1)} %get-tuple-element.81.grad_ref, bf16[4,384,1280]{2,1,0:T(8,128)(2,1)} %get-tuple-element.69.normed_ref), kind=kOutput, calls=%fused_computation.1 | convolution fusion | flops 3774873600 | bytes 11796480 | tf_op jit(solution)/shard_map/mbot,bti->moi/dot_general | solution.py:978
  189.2 6.7 %shard_map.212 = (bf16[2,384,1280]{2,1,0:T(8,128)(2,1)}, f32[8,1280]{1,0:T(8,128)}) custom-call(s32[13]{0:T(128)} %fusion.13.index_ref.place_ref.order_ref, bf16[3,4,320,384]{3,2,1,0:T(8,128)(2,1)} %get-tuple-element.81.grad_ref, bf16[6,320,1280]{2,1,0:T(8,128)(2,1)} %bitcast.69, bf16[384,1280]{1,0:T(8,128)(2,1)} %collective-permute-done.4.tok_b.refs_0_, ...), custom_call_target="tpu_custom_call" | custom-call | flops 3774873600 | bytes 6881280 | tf_op jit(solution)/shard_map/pallas_call | solution.py:733
  195.8 7.0 %shard_map.211 = (bf16[2,384,1280]{2,1,0:T(8,128)(2,1)}, f32[8,1280]{1,0:T(8,128)}) custom-call(s32[13]{0:T(128)} %fusion.13.index_ref.place_ref.order_ref, bf16[3,4,320,384]{3,2,1,0:T(8,128)(2,1)} %get-tuple-element.81.grad_ref, bf16[6,320,1280]{2,1,0:T(8,128)(2,1)} %bitcast.70, bf16[384,1280]{1,0:T(8,128)(2,1)} %tok_ref.3, ...), custom_call_target="tpu_custom_call" | custom-call | flops 3774873600 | bytes 6881280 | tf_op jit(solution)/shard_map/pallas_call | solution.py:733
  205.5 3.7 %collective-permute-done.29 = f32[8,6,320]{2,1,0:T(8,128)S(1)} collective-permute-done((f32[8,6,320]{2,1,0:T(8,128)S(1)}, f32[8,6,320]{2,1,0:T(8,128)S(1)}, u32[]{:S(2)}, u32[]{:S(2)}) %collective-permute-start.29) | collective-permute-done | bytes 61472 | tf_op jit(solution)/shard_map/ppermute | solution.py:44
  209.2 2.7 collective-permute-start.30
  213.4 3.3 %collective-permute-done.30 = f32[8,6,320]{2,1,0:T(8,128)S(1)} collective-permute-done((f32[8,6,320]{2,1,0:T(8,128)S(1)}, f32[8,6,320]{2,1,0:T(8,128)S(1)}, u32[]{:S(2)}, u32[]{:S(2)}) %collective-permute-start.30) | collective-permute-done | bytes 61472 | tf_op jit(solution)/shard_map/ppermute | solution.py:44
  217.4 2.8 shard_map.215.ortho_ref
  220.2 5.2 %shard_map.217 = bf16[3,8,1280]{2,1,0:T(8,128)(2,1)} custom-call(f32[6,8,320]{2,1,0:T(8,128)} %shard_map.215.ortho_ref, f32[6,320,1280]{2,1,0:T(8,128)} %bitcast.61, f32[3,320,1280]{2,1,0:T(8,128)} %convolution_bitcast_fusion.refs_1_), custom_call_target="tpu_custom_call" | custom-call | flops 39321600 | bytes 7372800 | tf_op jit(solution)/shard_map/pallas_call | solution.py:776
  226.0 18.6 %collective-permute-done.34 = f32[4,1280]{1,0:T(4,128)S(1)} collective-permute-done((f32[4,1280]{1,0:T(4,128)S(1)}, f32[4,1280]{1,0:T(4,128)S(1)}, u32[]{:S(2)}, u32[]{:S(2)}) %collective-permute-start.34) | collective-permute-done | bytes 20512 | tf_op jit(solution)/shard_map/ppermute | solution.py:40
  246.9 2.9 collective-permute-done.39
  249.9 2.7 collective-permute-start.40
  254.0 6.0 %shard_map.216 = bf16[3,8,1280]{2,1,0:T(8,128)(2,1)} custom-call(f32[6,8,320]{2,1,0:T(8,128)} %shard_map.215.ortho_ref, f32[6,320,1280]{2,1,0:T(8,128)} %bitcast.62, bf16[3,320,1280]{2,1,0:T(8,128)(2,1)} %get-tuple-element.87.refs_1_, bf16[3,320,1280]{2,1,0:T(8,128)(2,1)} %copy-done, bf16[3,320,1280]{2,1,0:T(8,128)(2,1)} %collective-permute-done.32.refs_3_), custom_call_target="tpu_custom_call" | custom-call | flops 39321600 | bytes 7372800 | tf_op jit(solution)/shard_map/pallas_call | solution.py:776
  262.3 3.1 %collective-permute-done.35 = bf16[26,1280]{1,0:T(8,128)(2,1)S(1)} collective-permute-done((bf16[26,1280]{1,0:T(8,128)(2,1)S(1)}, bf16[26,1280]{1,0:T(8,128)(2,1)S(1)}, u32[]{:S(2)}, u32[]{:S(2)}) %collective-permute-start.35) | collective-permute-done | bytes 66592 | tf_op jit(solution)/shard_map/ppermute | solution.py:44
  268.1 8.5 %shard_map.218 = (f32[6,320,1280]{2,1,0:T(8,128)}, f32[6,8,1280]{2,1,0:T(8,128)}, f32[6,160,320]{2,1,0:T(8,128)}, f32[6,160,320]{2,1,0:T(8,128)}, f32[6,160,320]{2,1,0:T(8,128)}) custom-call(f32[6,8,320]{2,1,0:T(8,128)} %shard_map.215.ortho_ref, f32[3,8,1280]{2,1,0:T(8,128)} %get-tuple-element.110.right_ref, ...), custom_call_target="tpu_custom_call" | custom-call | flops 58982400 | bytes 12288000 | tf_op jit(solution)/shard_map/pallas_call | solution.py:822
  279.1 3.9 %collective-permute-done.37 = bf16[26,1280]{1,0:T(8,128)(2,1)S(1)} collective-permute-done((bf16[26,1280]{1,0:T(8,128)(2,1)S(1)}, bf16[26,1280]{1,0:T(8,128)(2,1)S(1)}, u32[]{:S(2)}, u32[]{:S(2)}) %collective-permute-start.37) | collective-permute-done | bytes 66592 | tf_op jit(solution)/shard_map/ppermute | solution.py:44
  284.4 8.9 %shard_map.219 = (f32[6,320,1280]{2,1,0:T(8,128)}, f32[6,8,1280]{2,1,0:T(8,128)}, f32[6,160,320]{2,1,0:T(8,128)}, f32[6,160,320]{2,1,0:T(8,128)}, f32[6,160,320]{2,1,0:T(8,128)}) custom-call(f32[6,8,320]{2,1,0:T(8,128)} %shard_map.215.ortho_ref, ...), custom_call_target="tpu_custom_call", output_to_operand_aliasing={{0}: (8, {}), {1}: (9, {}), {2}: (10, {}), {3}: (11, {}), {... | custom-call | flops 58982400 | bytes 12288000 | tf_op jit(solution)/shard_map/pallas_call | solution.py:822
  294.0 4.5 %collective-permute-done.25.refs_0_ = bf16[384,1280]{1,0:T(8,128)(2,1)S(1)} collective-permute-done((bf16[384,1280]{1,0:T(8,128)(2,1)S(1)}, bf16[384,1280]{1,0:T(8,128)(2,1)S(1)}, u32[]{:S(2)}, u32[]{:S(2)}) %collective-permute-start.25) | collective-permute-done | bytes 983072 | tf_op jit(solution)/shard_map/ppermute | solution.py:40
  299.4 5.2 %shard_map.213 = f32[384,1280]{1,0:T(8,128)} custom-call(bf16[384,1280]{1,0:T(8,128)(2,1)} %tok_ref.3, f32[1,1280]{1,0:T(1,128)} %slice.86.gain_ref, f32[384,1280]{1,0:T(8,128)} %get-tuple-element.65.hidden_ref, bf16[2,384,1280]{2,1,0:T(8,128)(2,1)} %get-tuple-element.82.mine_ref, bf16[2,384,1280]{2,1,0:T(8,128)(2,1)} %collective-permute-done.24.paired_ref, ...), custom_call_target="tpu_custom_call" | custom-call | flops 9830400 | bytes 8847360 | tf_op jit(solution)/shard_map/pallas_call | solution.py:855
  (180 shorter events, 55.9 us)
Async XLA Ops:
  0.6 42.3 %collective-permute-start.4 = (bf16[384,1280]{1,0:T(8,128)(2,1)}, bf16[384,1280]{1,0:T(8,128)(2,1)}, u32[]{:S(2)}, u32[]{:S(2)}) collective-permute-start(bf16[384,1280]{1,0:T(8,128)(2,1)} %tok_ref.3), channel_id=1, source_target_pairs={{0,1},{1,0},{2,3},{3,2},{4,5},{5,4},{6,7},{7,6},{8,9},{9,8},{10,11... | collective-permute-start | bytes 2949128 | tf_op jit(solution)/shard_map/ppermute | solution.py:36
  1.2 25.5 %collective-permute-start.2 = (bf16[384,1280]{1,0:T(8,128)(2,1)}, bf16[384,1280]{1,0:T(8,128)(2,1)}, u32[]{:S(2)}, u32[]{:S(2)}) collective-permute-start(bf16[384,1280]{1,0:T(8,128)(2,1)} %tok_ref.3), channel_id=1, source_target_pairs={{0,2},{1,3},{2,0},{3,1},{4,6},{5,7},{6,4},{7,5},{8,10},{9,11},{10,... | collective-permute-start | bytes 2949128 | tf_op jit(solution)/shard_map/ppermute | solution.py:40
  4.6 22.4 %collective-permute-start = (bf16[5,1280]{1,0:T(8,128)(2,1)S(1)}, bf16[5,1280]{1,0:T(8,128)(2,1)S(1)}, u32[]{:S(2)}, u32[]{:S(2)}) collective-permute-start(bf16[5,1280]{1,0:T(8,128)(2,1)S(1)} %dynamic_update_slice.5), channel_id=1, source_target_pairs={{0,2},{1,3},{2,0},{3,1},{4,6},{5,7},{6,4},{7,5},{8,10},{9,11},{10,... | collective-permute-start | bytes 38408 | tf_op jit(solution)/shard_map/ppermute | solution.py:40
  6.7 33.6 %collective-permute-start.9 = (bf16[3,80,1280]{2,1,0:T(8,128)(2,1)}, bf16[3,80,1280]{2,1,0:T(8,128)(2,1)}, u32[]{:S(2)}, u32[]{:S(2)}) collective-permute-start(bf16[3,80,1280]{2,1,0:T(8,128)(2,1)} %dynamic-slice_bitcast_fusion), channel_id=1, source_target_pairs={{0,2},{1,3},{2,0},{3,1},{4,6},{5,7},{6,4},{7,5},{8,10},{9,11},{10,... | collective-permute-start | bytes 1843208 | tf_op jit(solution)/shard_map/ppermute | solution.py:40
  10.6 83.5 %collective-permute-start.8 = (bf16[3,320,1280]{2,1,0:T(8,128)(2,1)S(1)}, bf16[3,320,1280]{2,1,0:T(8,128)(2,1)}, u32[]{:S(2)}, u32[]{:S(2)}) collective-permute-start(bf16[3,320,1280]{2,1,0:T(8,128)(2,1)S(1)} %slice.88), channel_id=1, source_target_pairs={{0,1},{1,0},{2,3},{3,2},{4,5},{5,4},{6,7},{7,6},{8,9},{9,8},{10,11... | collective-permute-start | bytes 7372808 | tf_op jit(solution)/shard_map/ppermute | solution.py:36
  26.7 24.2 %collective-permute-start.3 = (bf16[384,1280]{1,0:T(8,128)(2,1)}, bf16[384,1280]{1,0:T(8,128)(2,1)S(1)}, u32[]{:S(2)}, u32[]{:S(2)}) collective-permute-start(bf16[384,1280]{1,0:T(8,128)(2,1)} %collective-permute-done.2.tok_a.refs_1_), channel_id=1, source_target_pairs={{0,1},{1,0},{2,3},{3,2},{4,5},{5,4},{6,7},{7,6},{8,9},{9,8},{10,11... | collective-permute-start | bytes 2949128 | tf_op jit(solution)/shard_map/ppermute | solution.py:36
  29.5 13.5 %collective-permute-start.20 = (bf16[48,1280]{1,0:T(8,128)(2,1)}, bf16[48,1280]{1,0:T(8,128)(2,1)S(1)}, u32[]{:S(2)}, u32[]{:S(2)}) collective-permute-start(bf16[48,1280]{1,0:T(8,128)(2,1)} %bitcast.81), channel_id=1, source_target_pairs={{0,2},{1,3},{2,0},{3,1},{4,6},{5,7},{6,4},{7,5},{8,10},{9,11},{10,... | collective-permute-start | bytes 368648 | tf_op jit(solution)/shard_map/ppermute | solution.py:40
  40.3 19.8 %collective-permute-start.10 = (bf16[1,3,80,1280]{3,2,1,0:T(8,128)(2,1)}, bf16[1,3,80,1280]{3,2,1,0:T(8,128)(2,1)}, u32[]{:S(2)}, u32[]{:S(2)}) collective-permute-start(bf16[1,3,80,1280]{3,2,1,0:T(8,128)(2,1)} %bitcast.4.refs_6_), channel_id=1, source_target_pairs={{0,4},{4,0},{8,12},{12,8},{16,20},{20,16},{24,28},{28,24},{1,5},{5... | collective-permute-start | bytes 1843208 | tf_op jit(solution)/shard_map/ppermute | solution.py:44
  42.9 17.1 %collective-permute-start.21 = (bf16[48,1280]{1,0:T(8,128)(2,1)}, bf16[48,1280]{1,0:T(8,128)(2,1)S(1)}, u32[]{:S(2)}, u32[]{:S(2)}) collective-permute-start(bf16[48,1280]{1,0:T(8,128)(2,1)} %bitcast.82), channel_id=1, source_target_pairs={{0,1},{1,0},{2,3},{3,2},{4,5},{5,4},{6,7},{7,6},{8,9},{9,8},{10,11... | collective-permute-start | bytes 368648 | tf_op jit(solution)/shard_map/ppermute | solution.py:36
  42.9 34.8 %collective-permute-start.22 = (bf16[48,1280]{1,0:T(8,128)(2,1)S(1)}, bf16[48,1280]{1,0:T(8,128)(2,1)S(1)}, u32[]{:S(2)}, u32[]{:S(2)}) collective-permute-start(bf16[48,1280]{1,0:T(8,128)(2,1)S(1)} %collective-permute-done.20), channel_id=1, source_target_pairs={{0,1},{1,0},{2,3},{3,2},{4,5},{5,4},{6,7},{7,6},{8,9},{9,8},{10,11... | collective-permute-start | bytes 368648 | tf_op jit(solution)/shard_map/ppermute | solution.py:36
  50.9 28.4 %collective-permute-start.11 = (bf16[1,3,80,1280]{3,2,1,0:T(8,128)(2,1)}, bf16[1,3,80,1280]{3,2,1,0:T(8,128)(2,1)}, u32[]{:S(2)}, u32[]{:S(2)}) collective-permute-start(bf16[1,3,80,1280]{3,2,1,0:T(8,128)(2,1)} %bitcast.4.refs_6_), channel_id=1, source_target_pairs={{0,8},{4,12},{8,0},{12,4},{16,24},{20,28},{24,16},{28,20},{1,9},{5... | collective-permute-start | bytes 1843208 | tf_op jit(solution)/shard_map/ppermute | solution.py:44
  60.0 19.3 %collective-permute-start.13 = (bf16[1,3,80,1280]{3,2,1,0:T(8,128)(2,1)}, bf16[1,3,80,1280]{3,2,1,0:T(8,128)(2,1)}, u32[]{:S(2)}, u32[]{:S(2)}) collective-permute-start(bf16[1,3,80,1280]{3,2,1,0:T(8,128)(2,1)} %bitcast.4.refs_6_), channel_id=1, source_target_pairs={{0,1},{1,0},{2,3},{3,2},{4,5},{5,4},{6,7},{7,6},{8,9},{9,8},{10,11... | collective-permute-start | bytes 1843208 | tf_op jit(solution)/shard_map/ppermute | solution.py:36
  60.1 20.2 %collective-permute-start.12 = (bf16[1,3,80,1280]{3,2,1,0:T(8,128)(2,1)}, bf16[1,3,80,1280]{3,2,1,0:T(8,128)(2,1)}, u32[]{:S(2)}, u32[]{:S(2)}) collective-permute-start(bf16[1,3,80,1280]{3,2,1,0:T(8,128)(2,1)} %collective-permute-done.10.refs_7_), channel_id=1, source_target_pairs={{0,8},{4,12},{8,0},{12,4},{16,24},{20,28},{24,16},{28,20},{1,9},{5... | collective-permute-start | bytes 1843208 | tf_op jit(solution)/shard_map/ppermute | solution.py:44
  77.7 13.6 %collective-permute-start.6 = (bf16[2,320,384]{2,1,0:T(8,128)(2,1)}, bf16[2,320,384]{2,1,0:T(8,128)(2,1)S(1)}, u32[]{:S(2)}, u32[]{:S(2)}) collective-permute-start(bf16[2,320,384]{2,1,0:T(8,128)(2,1)} %get-tuple-element.63), channel_id=1, source_target_pairs={{0,2},{1,3},{2,0},{3,1},{4,6},{5,7},{6,4},{7,5},{8,10},{9,11},{10,... | collective-permute-start | bytes 1474568 | tf_op jit(solution)/shard_map/ppermute | solution.py:40
  79.3 12.0 %collective-permute-start.15 = (bf16[1,3,80,1280]{3,2,1,0:T(8,128)(2,1)}, bf16[1,3,80,1280]{3,2,1,0:T(8,128)(2,1)S(1)}, u32[]{:S(2)}, u32[]{:S(2)}) collective-permute-start(bf16[1,3,80,1280]{3,2,1,0:T(8,128)(2,1)} %collective-permute-done.11.refs_8_), channel_id=1, source_target_pairs={{0,1},{1,0},{2,3},{3,2},{4,5},{5,4},{6,7},{7,6},{8,9},{9,8},{10,11... | collective-permute-start | bytes 1843208 | tf_op jit(solution)/shard_map/ppermute | solution.py:36
  79.3 14.7 %collective-permute-start.14 = (bf16[1,3,80,1280]{3,2,1,0:T(8,128)(2,1)}, bf16[1,3,80,1280]{3,2,1,0:T(8,128)(2,1)S(1)}, u32[]{:S(2)}, u32[]{:S(2)}) collective-permute-start(bf16[1,3,80,1280]{3,2,1,0:T(8,128)(2,1)} %collective-permute-done.10.refs_7_), channel_id=1, source_target_pairs={{0,1},{1,0},{2,3},{3,2},{4,5},{5,4},{6,7},{7,6},{8,9},{9,8},{10,11... | collective-permute-start | bytes 1843208 | tf_op jit(solution)/shard_map/ppermute | solution.py:36
  80.3 13.8 %collective-permute-start.16 = (bf16[1,3,80,1280]{3,2,1,0:T(8,128)(2,1)}, bf16[1,3,80,1280]{3,2,1,0:T(8,128)(2,1)S(1)}, u32[]{:S(2)}, u32[]{:S(2)}) collective-permute-start(bf16[1,3,80,1280]{3,2,1,0:T(8,128)(2,1)} %collective-permute-done.12.refs_9_), channel_id=1, source_target_pairs={{0,1},{1,0},{2,3},{3,2},{4,5},{5,4},{6,7},{7,6},{8,9},{9,8},{10,11... | collective-permute-start | bytes 1843208 | tf_op jit(solution)/shard_map/ppermute | solution.py:36
  130.2 20.7 %collective-permute-start.23 = (bf16[3,320,1280]{2,1,0:T(8,128)(2,1)}, bf16[3,320,1280]{2,1,0:T(8,128)(2,1)}, u32[]{:S(2)}, u32[]{:S(2)}) collective-permute-start(bf16[3,320,1280]{2,1,0:T(8,128)(2,1)} %get-tuple-element.76), channel_id=1, source_target_pairs={{0,1},{1,0},{2,3},{3,2},{4,5},{5,4},{6,7},{7,6},{8,9},{9,8},{10,11... | collective-permute-start | bytes 7372808 | tf_op jit(solution)/shard_map/ppermute | solution.py:36
  131.7 19.0 %collective-permute-start.18 = (bf16[2,320,384]{2,1,0:T(8,128)(2,1)}, bf16[2,320,384]{2,1,0:T(8,128)(2,1)S(1)}, u32[]{:S(2)}, u32[]{:S(2)}) collective-permute-start(bf16[2,320,384]{2,1,0:T(8,128)(2,1)} %get-tuple-element.72), channel_id=1, source_target_pairs={{0,2},{1,3},{2,0},{3,1},{4,6},{5,7},{6,4},{7,5},{8,10},{9,11},{10,... | collective-permute-start | bytes 1474568 | tf_op jit(solution)/shard_map/ppermute | solution.py:40
  136.2 14.5 %collective-permute-start.27 = (f32[3,8,320]{2,0,1:T(4,128)S(1)}, f32[3,8,320]{2,0,1:T(4,128)S(1)}, u32[]{:S(2)}, u32[]{:S(2)}) collective-permute-start(f32[3,8,320]{2,0,1:T(4,128)S(1)} %slice_bitcast_fusion.3), channel_id=1, source_target_pairs={{0,2},{1,3},{2,0},{3,1},{4,6},{5,7},{6,4},{7,5},{8,10},{9,11},{10,... | collective-permute-start | bytes 92168 | tf_op jit(solution)/shard_map/ppermute | solution.py:40
  150.3 102.2 %collective-permute-start.31 = (bf16[3,320,1280]{2,1,0:T(8,128)(2,1)}, bf16[3,320,1280]{2,1,0:T(8,128)(2,1)S(1)}, u32[]{:S(2)}, u32[]{:S(2)}) collective-permute-start(bf16[3,320,1280]{2,1,0:T(8,128)(2,1)} %get-tuple-element.88), channel_id=1, source_target_pairs={{0,1},{1,0},{2,3},{3,2},{4,5},{5,4},{6,7},{7,6},{8,9},{9,8},{10,11... | collective-permute-start | bytes 7372808 | tf_op jit(solution)/shard_map/ppermute | solution.py:36
  178.3 25.6 %collective-permute-start.28 = (f32[8,6,320]{2,1,0:T(8,128)S(1)}, f32[8,6,320]{2,1,0:T(8,128)S(1)}, u32[]{:S(2)}, u32[]{:S(2)}) collective-permute-start(f32[8,6,320]{2,1,0:T(8,128)S(1)} %fusion.4), channel_id=1, source_target_pairs={{0,4},{4,0},{8,12},{12,8},{16,20},{20,16},{24,28},{28,24},{1,5},{5... | collective-permute-start | bytes 184328 | tf_op jit(solution)/shard_map/ppermute | solution.py:44
  188.6 63.9 %collective-permute-start.32 = (bf16[3,320,1280]{2,1,0:T(8,128)(2,1)}, bf16[3,320,1280]{2,1,0:T(8,128)(2,1)}, u32[]{:S(2)}, u32[]{:S(2)}) collective-permute-start(bf16[3,320,1280]{2,1,0:T(8,128)(2,1)} %add_convert_fusion), channel_id=1, source_target_pairs={{0,2},{1,3},{2,0},{3,1},{4,6},{5,7},{6,4},{7,5},{8,10},{9,11},{10,... | collective-permute-start | bytes 7372808 | tf_op jit(solution)/shard_map/ppermute | solution.py:40
  203.7 8.2 %collective-permute-start.33 = (f32[4,1280]{1,0:T(4,128)S(1)}, f32[4,1280]{1,0:T(4,128)S(1)}, u32[]{:S(2)}, u32[]{:S(2)}) collective-permute-start(f32[4,1280]{1,0:T(4,128)S(1)} %pad_maximum_fusion.3), channel_id=1, source_target_pairs={{0,1},{1,0},{2,3},{3,2},{4,5},{5,4},{6,7},{7,6},{8,9},{9,8},{10,11... | collective-permute-start | bytes 61448 | tf_op jit(solution)/shard_map/ppermute | solution.py:36
  205.2 71.9 %collective-permute-start.24 = (bf16[2,384,1280]{2,1,0:T(8,128)(2,1)}, bf16[2,384,1280]{2,1,0:T(8,128)(2,1)}, u32[]{:S(2)}, u32[]{:S(2)}) collective-permute-start(bf16[2,384,1280]{2,1,0:T(8,128)(2,1)} %get-tuple-element.83), channel_id=1, source_target_pairs={{0,1},{1,0},{2,3},{3,2},{4,5},{5,4},{6,7},{7,6},{8,9},{9,8},{10,11... | collective-permute-start | bytes 5898248 | tf_op jit(solution)/shard_map/ppermute | solution.py:36
  209.2 7.5 %collective-permute-start.30 = (f32[8,6,320]{2,1,0:T(8,128)S(1)}, f32[8,6,320]{2,1,0:T(8,128)S(1)}, u32[]{:S(2)}, u32[]{:S(2)}) collective-permute-start(f32[8,6,320]{2,1,0:T(8,128)S(1)} %add.115), channel_id=1, source_target_pairs={{0,16},{4,20},{8,24},{12,28},{16,0},{20,4},{24,8},{28,12},{1,17},{... | collective-permute-start | bytes 184328 | tf_op jit(solution)/shard_map/ppermute | solution.py:44
  211.9 32.7 %collective-permute-start.34 = (f32[4,1280]{1,0:T(4,128)S(1)}, f32[4,1280]{1,0:T(4,128)S(1)}, u32[]{:S(2)}, u32[]{:S(2)}) collective-permute-start(f32[4,1280]{1,0:T(4,128)S(1)} %fusion.16), channel_id=1, source_target_pairs={{0,2},{1,3},{2,0},{3,1},{4,6},{5,7},{6,4},{7,5},{8,10},{9,11},{10,... | collective-permute-start | bytes 61448 | tf_op jit(solution)/shard_map/ppermute | solution.py:40
  225.4 19.3 %collective-permute-start.38 = (bf16[24,1280]{1,0:T(8,128)(2,1)}, bf16[24,1280]{1,0:T(8,128)(2,1)S(1)}, u32[]{:S(2)}, u32[]{:S(2)}) collective-permute-start(bf16[24,1280]{1,0:T(8,128)(2,1)} %bitcast.84), channel_id=1, source_target_pairs={{0,4},{4,0},{8,12},{12,8},{16,20},{20,16},{24,28},{28,24},{1,5},{5... | collective-permute-start | bytes 184328 | tf_op jit(solution)/shard_map/ppermute | solution.py:44
  249.9 11.7 %collective-permute-start.40 = (bf16[24,1280]{1,0:T(8,128)(2,1)S(1)}, bf16[24,1280]{1,0:T(8,128)(2,1)S(1)}, u32[]{:S(2)}, u32[]{:S(2)}) collective-permute-start(bf16[24,1280]{1,0:T(8,128)(2,1)S(1)} %add_convert_fusion.4), channel_id=1, source_target_pairs={{0,16},{4,20},{8,24},{12,28},{16,0},{20,4},{24,8},{28,12},{1,17},{... | collective-permute-start | bytes 184328 | tf_op jit(solution)/shard_map/ppermute | solution.py:44
  266.2 10.4 %collective-permute-start.36 = (bf16[26,1280]{1,0:T(8,128)(2,1)S(1)}, bf16[26,1280]{1,0:T(8,128)(2,1)S(1)}, u32[]{:S(2)}, u32[]{:S(2)}) collective-permute-start(bf16[26,1280]{1,0:T(8,128)(2,1)S(1)} %add_convert_fusion.3), channel_id=1, source_target_pairs={{0,8},{4,12},{8,0},{12,4},{16,24},{20,28},{24,16},{28,20},{1,9},{5... | collective-permute-start | bytes 199688 | tf_op jit(solution)/shard_map/ppermute | solution.py:44
  276.7 6.3 %collective-permute-start.37 = (bf16[26,1280]{1,0:T(8,128)(2,1)S(1)}, bf16[26,1280]{1,0:T(8,128)(2,1)S(1)}, u32[]{:S(2)}, u32[]{:S(2)}) collective-permute-start(bf16[26,1280]{1,0:T(8,128)(2,1)S(1)} %add_convert_fusion.2), channel_id=1, source_target_pairs={{0,16},{4,20},{8,24},{12,28},{16,0},{20,4},{24,8},{28,12},{1,17},{... | collective-permute-start | bytes 199688 | tf_op jit(solution)/shard_map/ppermute | solution.py:44
  278.5 19.9 %collective-permute-start.25 = (bf16[384,1280]{1,0:T(8,128)(2,1)S(1)}, bf16[384,1280]{1,0:T(8,128)(2,1)S(1)}, u32[]{:S(2)}, u32[]{:S(2)}) collective-permute-start(bf16[384,1280]{1,0:T(8,128)(2,1)S(1)} %fusion.1), channel_id=1, source_target_pairs={{0,2},{1,3},{2,0},{3,1},{4,6},{5,7},{6,4},{7,5},{8,10},{9,11},{10,... | collective-permute-start | bytes 2949128 | tf_op jit(solution)/shard_map/ppermute | solution.py:40
  (38 other events, 278.6 us)
where the time goes:
time: 306 us; the launch traced here: 305 us
  Pallas kernels  150 us (49%)
  waiting for transfers between devices  77.9 us (25%)
  starting transfers between devices  35.1 us (11%)
  other arithmetic  16.4 us (5%)
  local copies, waits for them, and re-layouts  15 us (5%)
  matrix products  8.83 us (3%)
    ppermute x10, waiting for transfers between devices, to_chip(): lax.ppermute(x, 'zero', [(i, (i + 2 * shift) % count) for i in range(coun...  57.5 us
    pallas_call x1, Pallas kernels, feed(): pl.pallas_call(feed_body, out_shape=(*[jax.ShapeDtypeStruct((own, rows),...  23.9 us
    pallas_call x1, Pallas kernels, attend_back(): pl.pallas_call(attend_back_body, out_shape=(jax.ShapeDtypeStruct((3, coun...  21 us
    ppermute x12, waiting for transfers between devices, to_rep(): return lax.ppermute(x, 'rep', [(i, i ^ step) for i in range(count)])  17.4 us
    pallas_call x2, Pallas kernels, finish(): pl.pallas_call(functools.partial(finish_body, rate, 1 + len(terms)), out_...  17.4 us
    ppermute x12, starting transfers between devices, to_rep(): return lax.ppermute(x, 'rep', [(i, i ^ step) for i in range(count)])  16.8 us
    pallas_call x1, Pallas kernels, attend(): pl.pallas_call(attend_body, out_shape=(*[jax.ShapeDtypeStruct((own, rows)...  16.7 us
    pallas_call x2, Pallas kernels, project(): pl.pallas_call(project_body, out_shape=shapes, grid_spec=pltpu.PrefetchSc...  14.9 us
  transfers between devices with their start and end apart: 41, of which 15 were waited for; matrix products, arithmetic and copies ran while one was open for 11% of the time, Pallas kernels for 36%

commit v1 on v0

--- a/solution.py
+++ b/solution.py
@@ -495,7 +495,7 @@
         hidden[:, lanes(j)] = part
         return square + jnp.sum(part * part, axis=-1, keepdims=True)
 
-    square = lax.fori_loop(0, tiles, first, jnp.zeros((rows, 1), f32))
+    square = lax.fori_loop(0, tiles, first, jnp.zeros((rows, 1), f32), unroll=True)
     scale = lax.rsqrt(square / width + EPS)
     normed = (hidden[...] * scale * vec_ref[1:2, :]).astype(bf16)
     inputs[1] = normed
@@ -517,7 +517,7 @@
         )
         return carry
 
-    lax.fori_loop(0, tiles, second, 0)
+    lax.fori_loop(0, tiles, second, 0, unroll=True)
     store(inputs.at[2], inputs_out.at[2])
     grad_up = result[...]
     grads[1] = grad_up.T
@@ -534,7 +534,7 @@
         weighted[:, lanes(j)] = turn
         return inner + jnp.sum(part * turn, axis=-1, keepdims=True)
 
-    inner = lax.fori_loop(0, tiles, third, jnp.zeros((rows, 1), f32)) / width
+    inner = lax.fori_loop(0, tiles, third, jnp.zeros((rows, 1), f32), unroll=True) / width
     store(result, result_out)
     back = cot_ref[...].astype(f32) + (
         scale * weighted[...] - hidden[...] * (scale * scale * scale) * inner
@@ -547,7 +547,7 @@
         att_grad[lanes(j), :] = dot(branch, w_cols(0, j), NN).astype(bf16).T
         return carry
 
-    lax.fori_loop(0, tiles, fourth, 0)
+    lax.fori_loop(0, tiles, fourth, 0, unroll=True)
     for p in range(count):
         target = att_grad_outs[p] if p < 2 else att_grad_outs[p // 2 + 1].at[p % 2]
         store(rows_of(att_grad, (p % 2) * (far + 1) + p // 2), target)
@@ -975,7 +975,7 @@
     toks = [tok_parts[i] for i in flipped]
     n1_away, gain_away = input_back(maps, 1, grads, w_mats, toks[chips:])
     n1_mine, gain_mine = input_back(maps, 0, grads, w_mats, toks[:chips])
-    near = jnp.einsum("mbot,bti->moi", grads, normed_all, preferred_element_type=f32)
+    near = jnp.einsum("mbot,bti->moi", grads, normed_all, preferred_element_type=f32).astype(bf16)
     n1_paired = to_pair(n1_away, n)
     n1_far = []
     for s in range(1, chips):

time: 306 us -> 298 us (0.974)
  Pallas kernels: 150 us -> 143 us
    pallas_call x1, Pallas kernels: 23.9 us -> 18.8 us  [feed(): pl.pallas_call(feed_body, out_shape=(*[jax.ShapeDtypeStruct((own, rows),...]
    ppermute x10, waiting for transfers between devices: 57.5 us -> 54.3 us  [to_chip(): lax.ppermute(x, 'zero', [(i, (i + 2 * shift) % count) for i in range(coun...]
  transfers between devices with their start and end apart: 41 -> 41, of which waited for: 15 -> 16; matrix products, arithmetic and copies ran while one was open for 11% -> 11% of each run, Pallas kernels for 36% -> 37%
where the time goes in v1:
time: 298 us; the launch traced here: 296 us
  Pallas kernels  143 us (48%)
  waiting for transfers between devices  77 us (26%)
  starting transfers between devices  36.6 us (12%)
  other arithmetic  15.6 us (5%)
  local copies, waits for them, and re-layouts  14.1 us (5%)
  matrix products  7.87 us (3%)
    ppermute x10, waiting for transfers between devices, to_chip(): lax.ppermute(x, 'zero', [(i, (i + 2 * shift) % count) for i in range(coun...  54.3 us
    pallas_call x1, Pallas kernels, attend_back(): pl.pallas_call(attend_back_body, out_shape=(jax.ShapeDtypeStruct((3, coun...  21.4 us
    ppermute x12, waiting for transfers between devices, to_rep(): return lax.ppermute(x, 'rep', [(i, i ^ step) for i in range(count)])  19 us
    pallas_call x1, Pallas kernels, feed(): pl.pallas_call(feed_body, out_shape=(*[jax.ShapeDtypeStruct((own, rows),...  18.8 us
    ppermute x12, starting transfers between devices, to_rep(): return lax.ppermute(x, 'rep', [(i, i ^ step) for i in range(count)])  18.3 us
    pallas_call x2, Pallas kernels, finish(): pl.pallas_call(functools.partial(finish_body, rate, 1 + len(terms)), out_...  16.7 us
    pallas_call x1, Pallas kernels, attend(): pl.pallas_call(attend_body, out_shape=(*[jax.ShapeDtypeStruct((own, rows)...  16.7 us
    pallas_call x2, Pallas kernels, project(): pl.pallas_call(project_body, out_shape=shapes, grid_spec=pltpu.PrefetchSc...  14.9 us
  transfers between devices with their start and end apart: 41, of which 16 were waited for; matrix products, arithmetic and copies ran while one was open for 11% of the time, Pallas kernels for 37%

profile of v1, /device:TPU:0, one launch (start us, length us, event | category | flops | bytes accessed | tf_op | source)
XLA Modules:
  0.0 296.4 jit_solution(17607142001759268289)
XLA Ops:
  1.2 2.6 collective-permute-start.2
  12.3 14.3 %collective-permute-done.2.tok_a.refs_1_ = bf16[384,1280]{1,0:T(8,128)(2,1)} collective-permute-done((bf16[384,1280]{1,0:T(8,128)(2,1)}, bf16[384,1280]{1,0:T(8,128)(2,1)}, u32[]{:S(2)}, u32[]{:S(2)}) %collective-permute-start.2) | collective-permute-done | bytes 983072 | tf_op jit(solution)/shard_map/ppermute | solution.py:40
  31.5 8.8 %collective-permute-done.9 = bf16[3,80,1280]{2,1,0:T(8,128)(2,1)} collective-permute-done((bf16[3,80,1280]{2,1,0:T(8,128)(2,1)}, bf16[3,80,1280]{2,1,0:T(8,128)(2,1)}, u32[]{:S(2)}, u32[]{:S(2)}) %collective-permute-start.9) | collective-permute-done | bytes 614432 | tf_op jit(solution)/shard_map/ppermute | solution.py:40
  43.5 7.4 %shard_map.204 = (bf16[4,384,1280]{2,1,0:T(8,128)(2,1)}, bf16[4,960,384]{2,1,0:T(8,128)(2,1)}, bf16[4,320,384]{2,1,0:T(8,128)(2,1)}) custom-call(s32[13]{0:T(128)} %fusion.13.index_ref.place_ref.order_ref, bf16[384,1280]{1,0:T(8,128)(2,1)} %tok_ref.3, bf16[384,1280]{1,0:T(8,128)(2,1)} %collective-permute-done.4.tok_b.refs_0_, f32[1,1280]{1,0:T(1,128)} %slice.86.gain_ref, ...), custom_call_target="tpu_custom_call" | custom-call | flops 1887436800 | bytes 6389760 | tf_op jit(solution)/shard_map/pallas_call | solution.py:155
  52.6 7.4 %shard_map.205 = (bf16[4,384,1280]{2,1,0:T(8,128)(2,1)}, bf16[4,960,384]{2,1,0:T(8,128)(2,1)}, bf16[4,320,384]{2,1,0:T(8,128)(2,1)}) custom-call(s32[13]{0:T(128)} %fusion.13.index_ref.place_ref.order_ref, bf16[384,1280]{1,0:T(8,128)(2,1)} %collective-permute-done.2.tok_a.refs_1_, ...), custom_call_target="tpu_custom_call", output_to_operand_aliasing={{0}: (6, {}), {1}: (7, {}), {2}: (8, {})} | custom-call | flops 1887436800 | bytes 6389760 | tf_op jit(solution)/shard_map/pallas_call | solution.py:155
  61.0 16.7 %shard_map.206 = (bf16[320,384]{1,0:T(8,128)(2,1)}, bf16[320,384]{1,0:T(8,128)(2,1)}, bf16[2,320,384]{2,1,0:T(8,128)(2,1)}, bf16[4,320,384]{2,1,0:T(8,128)(2,1)}, f32[4,4,384]{2,1,0:T(4,128)}) custom-call(s32[1]{0:T(128)S(6)} %copy.71.valid_ref, s32[13]{0:T(128)} %fusion.13.index_ref.place_ref.order_ref, ...), custom_call_target="tpu_custom_call" | custom-call | flops 4294967296 | bytes 4423680 | tf_op jit(solution)/shard_map/pallas_call | solution.py:249
  80.3 11.0 %collective-permute-done.6.refs_2_ = bf16[2,320,384]{2,1,0:T(8,128)(2,1)S(1)} collective-permute-done((bf16[2,320,384]{2,1,0:T(8,128)(2,1)}, bf16[2,320,384]{2,1,0:T(8,128)(2,1)S(1)}, u32[]{:S(2)}, u32[]{:S(2)}) %collective-permute-start.6) | collective-permute-done | bytes 491552 | tf_op jit(solution)/shard_map/ppermute | solution.py:40
  95.8 18.8 %shard_map.207 = (bf16[320,384]{1,0:T(8,128)(2,1)}, bf16[320,384]{1,0:T(8,128)(2,1)}, bf16[2,320,384]{2,1,0:T(8,128)(2,1)}, bf16[384,1280]{1,0:T(8,128)(2,1)}, f...) custom-call(s32[13]{0:T(128)} %fusion.13.index_ref.place_ref.order_ref, ...), custom_call_target="tpu_custom_call" | custom-call | flops 7549747200 | bytes 21626880 | tf_op jit(solution)/shard_map/pallas_call | solution.py:565
  114.6 10.6 %shard_map.209 = (bf16[3,320,1280]{2,1,0:T(8,128)(2,1)}, bf16[3,320,1280]{2,1,0:T(8,128)(2,1)}, bf16[3,320,1280]{2,1,0:T(8,128)(2,1)}, bf16[3,320,1280]{2,1,0:T(...) custom-call(bf16[3,4,320,384]{3,2,1,0:T(8,128)(2,1)} %get-tuple-element.73.grad_ref, ...), custom_call_target="tpu_custom_call" | custom-call | flops 3774873600 | bytes 25559040 | tf_op jit(solution)/shard_map/pallas_call | solution.py:638
  132.8 7.7 %shard_map.214 = f32[6,8,320]{2,1,0:T(8,128)} custom-call(f32[6,320,1280]{2,1,0:T(8,128)} %bitcast.60, f32[6,8,1280]{2,1,0:T(8,128)} %bitcast.74), custom_call_target="tpu_custom_call" | custom-call | flops 78643200 | bytes 9830400 | tf_op jit(solution)/shard_map/pallas_call | solution.py:692
  140.5 4.7 %shard_map.208.spread_ref = bf16[4,48,384]{2,1,0:T(8,128)(2,1)} custom-call(bf16[4,384,1280]{2,1,0:T(8,128)(2,1)} %get-tuple-element.69.normed_ref, bf16[48,1280]{1,0:T(8,128)(2,1)} %bitcast.80), custom_call_target="tpu_custom_call" | custom-call | flops 188743680 | bytes 3932160 | tf_op jit(solution)/shard_map/pallas_call | solution.py:665
  146.0 3.6 %add_convert_fusion = bf16[3,320,1280]{2,1,0:T(8,128)(2,1)} fusion(bf16[3,320,1280]{2,1,0:T(8,128)(2,1)} %collective-permute-done.23, bf16[3,320,1280]{2,1,0:T(8,128)(2,1)S(1)} %copy-done.3), kind=kLoop, calls=%fused_computation.1 | loop fusion | flops 4915200 | bytes 7372800 | tf_op jit(solution)/shard_map/convert_element_type | solution.py:953
  151.3 21.4 %shard_map.210 = (bf16[3,4,320,384]{3,2,1,0:T(8,128)(2,1)}, f32[320,128]{1,0:T(8,128)}, f32[4,3,8,128]{3,2,1,0:T(8,128)}) custom-call(s32[1]{0:T(128)S(6)} %copy.71.valid_ref, s32[13]{0:T(128)} %fusion.13.index_ref.place_ref.order_ref, bf16[4,960,384]{2,1,0:T(8,128)(2,1)} %get-tuple-element.60.q_ref.k_ref.v_ref, ...), custom_call_target="tpu_custom_call" | custom-call | flops 10737418240 | bytes 7372800 | tf_op jit(solution)/shard_map/pallas_call | solution.py:358
  172.8 7.9 %bitcast_convert_fusion.refs_1_ = bf16[3,320,1280]{2,1,0:T(8,128)(2,1)} fusion(bf16[3,4,320,384]{3,2,1,0:T(8,128)(2,1)} %get-tuple-element.81.grad_ref, bf16[4,384,1280]{2,1,0:T(8,128)(2,1)S(1)} %copy-done), kind=kOutput, calls=%fused_computation | convolution fusion | flops 3776102400 | bytes 9338880 | tf_op jit(solution)/shard_map/mbot,bti->moi/dot_general | solution.py:978
  181.2 6.7 %shard_map.212 = (bf16[2,384,1280]{2,1,0:T(8,128)(2,1)}, f32[8,1280]{1,0:T(8,128)}) custom-call(s32[13]{0:T(128)} %fusion.13.index_ref.place_ref.order_ref, bf16[3,4,320,384]{3,2,1,0:T(8,128)(2,1)} %get-tuple-element.81.grad_ref, bf16[6,320,1280]{2,1,0:T(8,128)(2,1)} %bitcast.69, bf16[384,1280]{1,0:T(8,128)(2,1)} %collective-permute-done.4.tok_b.refs_0_, ...), custom_call_target="tpu_custom_call" | custom-call | flops 3774873600 | bytes 6881280 | tf_op jit(solution)/shard_map/pallas_call | solution.py:733
  187.9 6.8 %shard_map.211 = (bf16[2,384,1280]{2,1,0:T(8,128)(2,1)}, f32[8,1280]{1,0:T(8,128)}) custom-call(s32[13]{0:T(128)} %fusion.13.index_ref.place_ref.order_ref, bf16[3,4,320,384]{3,2,1,0:T(8,128)(2,1)} %get-tuple-element.81.grad_ref, bf16[6,320,1280]{2,1,0:T(8,128)(2,1)} %bitcast.70, bf16[384,1280]{1,0:T(8,128)(2,1)} %tok_ref.3, ...), custom_call_target="tpu_custom_call" | custom-call | flops 3774873600 | bytes 6881280 | tf_op jit(solution)/shard_map/pallas_call | solution.py:733
  197.5 3.6 %collective-permute-done.28 = f32[8,6,320]{2,1,0:T(8,128)S(1)} collective-permute-done((f32[8,6,320]{2,1,0:T(8,128)S(1)}, f32[8,6,320]{2,1,0:T(8,128)S(1)}, u32[]{:S(2)}, u32[]{:S(2)}) %collective-permute-start.28) | collective-permute-done | bytes 61472 | tf_op jit(solution)/shard_map/ppermute | solution.py:44
  202.4 3.4 %collective-permute-done.29 = f32[8,6,320]{2,1,0:T(8,128)S(1)} collective-permute-done((f32[8,6,320]{2,1,0:T(8,128)S(1)}, f32[8,6,320]{2,1,0:T(8,128)S(1)}, u32[]{:S(2)}, u32[]{:S(2)}) %collective-permute-start.29) | collective-permute-done | bytes 61472 | tf_op jit(solution)/shard_map/ppermute | solution.py:44
  205.8 2.7 collective-permute-start.30
  210.0 2.4 collective-permute-done.30
  213.1 2.8 shard_map.215.ortho_ref
  215.9 4.6 %shard_map.217 = bf16[3,8,1280]{2,1,0:T(8,128)(2,1)} custom-call(f32[6,8,320]{2,1,0:T(8,128)} %shard_map.215.ortho_ref, f32[6,320,1280]{2,1,0:T(8,128)} %bitcast.61, bf16[3,320,1280]{2,1,0:T(8,128)(2,1)} %bitcast_convert_fusion.refs_1_), custom_call_target="tpu_custom_call" | custom-call | flops 39321600 | bytes 7372800 | tf_op jit(solution)/shard_map/pallas_call | solution.py:776
  221.8 15.2 %collective-permute-done.34 = f32[4,1280]{1,0:T(4,128)S(1)} collective-permute-done((f32[4,1280]{1,0:T(4,128)S(1)}, f32[4,1280]{1,0:T(4,128)S(1)}, u32[]{:S(2)}, u32[]{:S(2)}) %collective-permute-start.34) | collective-permute-done | bytes 20512 | tf_op jit(solution)/shard_map/ppermute | solution.py:40
  239.3 2.9 collective-permute-done.39
  242.2 2.6 collective-permute-start.40
  246.3 6.0 %shard_map.216 = bf16[3,8,1280]{2,1,0:T(8,128)(2,1)} custom-call(f32[6,8,320]{2,1,0:T(8,128)} %shard_map.215.ortho_ref, f32[6,320,1280]{2,1,0:T(8,128)} %bitcast.62, bf16[3,320,1280]{2,1,0:T(8,128)(2,1)} %get-tuple-element.87.refs_1_, bf16[3,320,1280]{2,1,0:T(8,128)(2,1)} %collective-permute-done.31.refs_2_, bf16[3,320,1280]{2,1,0:T(8,128)(2,1)} %copy-done.1), custom_call_target="tpu_custom_call" | custom-call | flops 39321600 | bytes 7372800 | tf_op jit(solution)/shard_map/pallas_call | solution.py:776
  255.2 2.4 collective-permute-done.35
  260.4 7.8 %shard_map.218 = (f32[6,320,1280]{2,1,0:T(8,128)}, f32[6,8,1280]{2,1,0:T(8,128)}, f32[6,160,320]{2,1,0:T(8,128)}, f32[6,160,320]{2,1,0:T(8,128)}, f32[6,160,320]{2,1,0:T(8,128)}) custom-call(f32[6,8,320]{2,1,0:T(8,128)} %shard_map.215.ortho_ref, f32[3,8,1280]{2,1,0:T(8,128)} %get-tuple-element.110.right_ref, ...), custom_call_target="tpu_custom_call" | custom-call | flops 58982400 | bytes 12288000 | tf_op jit(solution)/shard_map/pallas_call | solution.py:822
  270.7 3.8 %collective-permute-done.37 = bf16[26,1280]{1,0:T(8,128)(2,1)S(1)} collective-permute-done((bf16[26,1280]{1,0:T(8,128)(2,1)S(1)}, bf16[26,1280]{1,0:T(8,128)(2,1)S(1)}, u32[]{:S(2)}, u32[]{:S(2)}) %collective-permute-start.37) | collective-permute-done | bytes 66592 | tf_op jit(solution)/shard_map/ppermute | solution.py:44
  276.0 8.9 %shard_map.219 = (f32[6,320,1280]{2,1,0:T(8,128)}, f32[6,8,1280]{2,1,0:T(8,128)}, f32[6,160,320]{2,1,0:T(8,128)}, f32[6,160,320]{2,1,0:T(8,128)}, f32[6,160,320]{2,1,0:T(8,128)}) custom-call(f32[6,8,320]{2,1,0:T(8,128)} %shard_map.215.ortho_ref, ...), custom_call_target="tpu_custom_call", output_to_operand_aliasing={{0}: (8, {}), {1}: (9, {}), {2}: (10, {}), {3}: (11, {}), {... | custom-call | flops 58982400 | bytes 12288000 | tf_op jit(solution)/shard_map/pallas_call | solution.py:822
  285.6 4.6 %collective-permute-done.25.refs_0_ = bf16[384,1280]{1,0:T(8,128)(2,1)S(1)} collective-permute-done((bf16[384,1280]{1,0:T(8,128)(2,1)S(1)}, bf16[384,1280]{1,0:T(8,128)(2,1)S(1)}, u32[]{:S(2)}, u32[]{:S(2)}) %collective-permute-start.25) | collective-permute-done | bytes 983072 | tf_op jit(solution)/shard_map/ppermute | solution.py:40
  291.2 5.2 %shard_map.213 = f32[384,1280]{1,0:T(8,128)} custom-call(bf16[384,1280]{1,0:T(8,128)(2,1)} %tok_ref.3, f32[1,1280]{1,0:T(1,128)} %slice.86.gain_ref, f32[384,1280]{1,0:T(8,128)} %get-tuple-element.65.hidden_ref, bf16[2,384,1280]{2,1,0:T(8,128)(2,1)} %get-tuple-element.82.mine_ref, bf16[2,384,1280]{2,1,0:T(8,128)(2,1)} %collective-permute-done.24.paired_ref, ...), custom_call_target="tpu_custom_call" | custom-call | flops 9830400 | bytes 8847360 | tf_op jit(solution)/shard_map/pallas_call | solution.py:855
  (186 shorter events, 59.4 us)
Async XLA Ops:
  0.6 42.3 %collective-permute-start.4 = (bf16[384,1280]{1,0:T(8,128)(2,1)}, bf16[384,1280]{1,0:T(8,128)(2,1)}, u32[]{:S(2)}, u32[]{:S(2)}) collective-permute-start(bf16[384,1280]{1,0:T(8,128)(2,1)} %tok_ref.3), channel_id=1, source_target_pairs={{0,1},{1,0},{2,3},{3,2},{4,5},{5,4},{6,7},{7,6},{8,9},{9,8},{10,11... | collective-permute-start | bytes 2949128 | tf_op jit(solution)/shard_map/ppermute | solution.py:36
  1.2 25.5 %collective-permute-start.2 = (bf16[384,1280]{1,0:T(8,128)(2,1)}, bf16[384,1280]{1,0:T(8,128)(2,1)}, u32[]{:S(2)}, u32[]{:S(2)}) collective-permute-start(bf16[384,1280]{1,0:T(8,128)(2,1)} %tok_ref.3), channel_id=1, source_target_pairs={{0,2},{1,3},{2,0},{3,1},{4,6},{5,7},{6,4},{7,5},{8,10},{9,11},{10,... | collective-permute-start | bytes 2949128 | tf_op jit(solution)/shard_map/ppermute | solution.py:40
  4.6 22.4 %collective-permute-start = (bf16[5,1280]{1,0:T(8,128)(2,1)S(1)}, bf16[5,1280]{1,0:T(8,128)(2,1)S(1)}, u32[]{:S(2)}, u32[]{:S(2)}) collective-permute-start(bf16[5,1280]{1,0:T(8,128)(2,1)S(1)} %dynamic_update_slice.5), channel_id=1, source_target_pairs={{0,2},{1,3},{2,0},{3,1},{4,6},{5,7},{6,4},{7,5},{8,10},{9,11},{10,... | collective-permute-start | bytes 38408 | tf_op jit(solution)/shard_map/ppermute | solution.py:40
  6.7 33.6 %collective-permute-start.9 = (bf16[3,80,1280]{2,1,0:T(8,128)(2,1)}, bf16[3,80,1280]{2,1,0:T(8,128)(2,1)}, u32[]{:S(2)}, u32[]{:S(2)}) collective-permute-start(bf16[3,80,1280]{2,1,0:T(8,128)(2,1)} %dynamic-slice_bitcast_fusion), channel_id=1, source_target_pairs={{0,2},{1,3},{2,0},{3,1},{4,6},{5,7},{6,4},{7,5},{8,10},{9,11},{10,... | collective-permute-start | bytes 1843208 | tf_op jit(solution)/shard_map/ppermute | solution.py:40
  10.6 83.4 %collective-permute-start.8 = (bf16[3,320,1280]{2,1,0:T(8,128)(2,1)S(1)}, bf16[3,320,1280]{2,1,0:T(8,128)(2,1)}, u32[]{:S(2)}, u32[]{:S(2)}) collective-permute-start(bf16[3,320,1280]{2,1,0:T(8,128)(2,1)S(1)} %slice.88), channel_id=1, source_target_pairs={{0,1},{1,0},{2,3},{3,2},{4,5},{5,4},{6,7},{7,6},{8,9},{9,8},{10,11... | collective-permute-start | bytes 7372808 | tf_op jit(solution)/shard_map/ppermute | solution.py:36
  26.7 24.2 %collective-permute-start.3 = (bf16[384,1280]{1,0:T(8,128)(2,1)}, bf16[384,1280]{1,0:T(8,128)(2,1)S(1)}, u32[]{:S(2)}, u32[]{:S(2)}) collective-permute-start(bf16[384,1280]{1,0:T(8,128)(2,1)} %collective-permute-done.2.tok_a.refs_1_), channel_id=1, source_target_pairs={{0,1},{1,0},{2,3},{3,2},{4,5},{5,4},{6,7},{7,6},{8,9},{9,8},{10,11... | collective-permute-start | bytes 2949128 | tf_op jit(solution)/shard_map/ppermute | solution.py:36
  29.5 13.5 %collective-permute-start.20 = (bf16[48,1280]{1,0:T(8,128)(2,1)}, bf16[48,1280]{1,0:T(8,128)(2,1)S(1)}, u32[]{:S(2)}, u32[]{:S(2)}) collective-permute-start(bf16[48,1280]{1,0:T(8,128)(2,1)} %bitcast.81), channel_id=1, source_target_pairs={{0,2},{1,3},{2,0},{3,1},{4,6},{5,7},{6,4},{7,5},{8,10},{9,11},{10,... | collective-permute-start | bytes 368648 | tf_op jit(solution)/shard_map/ppermute | solution.py:40
  40.3 19.8 %collective-permute-start.10 = (bf16[1,3,80,1280]{3,2,1,0:T(8,128)(2,1)}, bf16[1,3,80,1280]{3,2,1,0:T(8,128)(2,1)}, u32[]{:S(2)}, u32[]{:S(2)}) collective-permute-start(bf16[1,3,80,1280]{3,2,1,0:T(8,128)(2,1)} %bitcast.4.refs_6_), channel_id=1, source_target_pairs={{0,4},{4,0},{8,12},{12,8},{16,20},{20,16},{24,28},{28,24},{1,5},{5... | collective-permute-start | bytes 1843208 | tf_op jit(solution)/shard_map/ppermute | solution.py:44
  42.9 17.1 %collective-permute-start.21 = (bf16[48,1280]{1,0:T(8,128)(2,1)}, bf16[48,1280]{1,0:T(8,128)(2,1)S(1)}, u32[]{:S(2)}, u32[]{:S(2)}) collective-permute-start(bf16[48,1280]{1,0:T(8,128)(2,1)} %bitcast.82), channel_id=1, source_target_pairs={{0,1},{1,0},{2,3},{3,2},{4,5},{5,4},{6,7},{7,6},{8,9},{9,8},{10,11... | collective-permute-start | bytes 368648 | tf_op jit(solution)/shard_map/ppermute | solution.py:36
  43.0 34.8 %collective-permute-start.22 = (bf16[48,1280]{1,0:T(8,128)(2,1)S(1)}, bf16[48,1280]{1,0:T(8,128)(2,1)}, u32[]{:S(2)}, u32[]{:S(2)}) collective-permute-start(bf16[48,1280]{1,0:T(8,128)(2,1)S(1)} %collective-permute-done.20), channel_id=1, source_target_pairs={{0,1},{1,0},{2,3},{3,2},{4,5},{5,4},{6,7},{7,6},{8,9},{9,8},{10,11... | collective-permute-start | bytes 368648 | tf_op jit(solution)/shard_map/ppermute | solution.py:36
  50.9 28.4 %collective-permute-start.11 = (bf16[1,3,80,1280]{3,2,1,0:T(8,128)(2,1)}, bf16[1,3,80,1280]{3,2,1,0:T(8,128)(2,1)}, u32[]{:S(2)}, u32[]{:S(2)}) collective-permute-start(bf16[1,3,80,1280]{3,2,1,0:T(8,128)(2,1)} %bitcast.4.refs_6_), channel_id=1, source_target_pairs={{0,8},{4,12},{8,0},{12,4},{16,24},{20,28},{24,16},{28,20},{1,9},{5... | collective-permute-start | bytes 1843208 | tf_op jit(solution)/shard_map/ppermute | solution.py:44
  60.0 19.3 %collective-permute-start.13 = (bf16[1,3,80,1280]{3,2,1,0:T(8,128)(2,1)}, bf16[1,3,80,1280]{3,2,1,0:T(8,128)(2,1)}, u32[]{:S(2)}, u32[]{:S(2)}) collective-permute-start(bf16[1,3,80,1280]{3,2,1,0:T(8,128)(2,1)} %bitcast.4.refs_6_), channel_id=1, source_target_pairs={{0,1},{1,0},{2,3},{3,2},{4,5},{5,4},{6,7},{7,6},{8,9},{9,8},{10,11... | collective-permute-start | bytes 1843208 | tf_op jit(solution)/shard_map/ppermute | solution.py:36
  60.1 20.2 %collective-permute-start.12 = (bf16[1,3,80,1280]{3,2,1,0:T(8,128)(2,1)}, bf16[1,3,80,1280]{3,2,1,0:T(8,128)(2,1)}, u32[]{:S(2)}, u32[]{:S(2)}) collective-permute-start(bf16[1,3,80,1280]{3,2,1,0:T(8,128)(2,1)} %collective-permute-done.10.refs_7_), channel_id=1, source_target_pairs={{0,8},{4,12},{8,0},{12,4},{16,24},{20,28},{24,16},{28,20},{1,9},{5... | collective-permute-start | bytes 1843208 | tf_op jit(solution)/shard_map/ppermute | solution.py:44
  77.7 13.6 %collective-permute-start.6 = (bf16[2,320,384]{2,1,0:T(8,128)(2,1)}, bf16[2,320,384]{2,1,0:T(8,128)(2,1)S(1)}, u32[]{:S(2)}, u32[]{:S(2)}) collective-permute-start(bf16[2,320,384]{2,1,0:T(8,128)(2,1)} %get-tuple-element.63), channel_id=1, source_target_pairs={{0,2},{1,3},{2,0},{3,1},{4,6},{5,7},{6,4},{7,5},{8,10},{9,11},{10,... | collective-permute-start | bytes 1474568 | tf_op jit(solution)/shard_map/ppermute | solution.py:40
  79.3 12.0 %collective-permute-start.15 = (bf16[1,3,80,1280]{3,2,1,0:T(8,128)(2,1)}, bf16[1,3,80,1280]{3,2,1,0:T(8,128)(2,1)S(1)}, u32[]{:S(2)}, u32[]{:S(2)}) collective-permute-start(bf16[1,3,80,1280]{3,2,1,0:T(8,128)(2,1)} %collective-permute-done.11.refs_8_), channel_id=1, source_target_pairs={{0,1},{1,0},{2,3},{3,2},{4,5},{5,4},{6,7},{7,6},{8,9},{9,8},{10,11... | collective-permute-start | bytes 1843208 | tf_op jit(solution)/shard_map/ppermute | solution.py:36
  79.3 14.7 %collective-permute-start.14 = (bf16[1,3,80,1280]{3,2,1,0:T(8,128)(2,1)}, bf16[1,3,80,1280]{3,2,1,0:T(8,128)(2,1)S(1)}, u32[]{:S(2)}, u32[]{:S(2)}) collective-permute-start(bf16[1,3,80,1280]{3,2,1,0:T(8,128)(2,1)} %collective-permute-done.10.refs_7_), channel_id=1, source_target_pairs={{0,1},{1,0},{2,3},{3,2},{4,5},{5,4},{6,7},{7,6},{8,9},{9,8},{10,11... | collective-permute-start | bytes 1843208 | tf_op jit(solution)/shard_map/ppermute | solution.py:36
  80.3 13.7 %collective-permute-start.16 = (bf16[1,3,80,1280]{3,2,1,0:T(8,128)(2,1)}, bf16[1,3,80,1280]{3,2,1,0:T(8,128)(2,1)S(1)}, u32[]{:S(2)}, u32[]{:S(2)}) collective-permute-start(bf16[1,3,80,1280]{3,2,1,0:T(8,128)(2,1)} %collective-permute-done.12.refs_9_), channel_id=1, source_target_pairs={{0,1},{1,0},{2,3},{3,2},{4,5},{5,4},{6,7},{7,6},{8,9},{9,8},{10,11... | collective-permute-start | bytes 1843208 | tf_op jit(solution)/shard_map/ppermute | solution.py:36
  125.1 20.9 %collective-permute-start.23 = (bf16[3,320,1280]{2,1,0:T(8,128)(2,1)}, bf16[3,320,1280]{2,1,0:T(8,128)(2,1)}, u32[]{:S(2)}, u32[]{:S(2)}) collective-permute-start(bf16[3,320,1280]{2,1,0:T(8,128)(2,1)} %get-tuple-element.76), channel_id=1, source_target_pairs={{0,1},{1,0},{2,3},{3,2},{4,5},{5,4},{6,7},{7,6},{8,9},{9,8},{10,11... | collective-permute-start | bytes 7372808 | tf_op jit(solution)/shard_map/ppermute | solution.py:36
  126.7 19.1 %collective-permute-start.18 = (bf16[2,320,384]{2,1,0:T(8,128)(2,1)S(1)}, bf16[2,320,384]{2,1,0:T(8,128)(2,1)S(1)}, u32[]{:S(2)}, u32[]{:S(2)}) collective-permute-start(bf16[2,320,384]{2,1,0:T(8,128)(2,1)S(1)} %copy-done.26), channel_id=1, source_target_pairs={{0,2},{1,3},{2,0},{3,1},{4,6},{5,7},{6,4},{7,5},{8,10},{9,11},{10,... | collective-permute-start | bytes 1474568 | tf_op jit(solution)/shard_map/ppermute | solution.py:40
  131.2 14.6 %collective-permute-start.27 = (f32[3,8,320]{2,0,1:T(4,128)S(1)}, f32[3,8,320]{2,0,1:T(4,128)S(1)}, u32[]{:S(2)}, u32[]{:S(2)}) collective-permute-start(f32[3,8,320]{2,0,1:T(4,128)S(1)} %slice_bitcast_fusion.3), channel_id=1, source_target_pairs={{0,2},{1,3},{2,0},{3,1},{4,6},{5,7},{6,4},{7,5},{8,10},{9,11},{10,... | collective-permute-start | bytes 92168 | tf_op jit(solution)/shard_map/ppermute | solution.py:40
  145.4 99.5 %collective-permute-start.31 = (bf16[3,320,1280]{2,1,0:T(8,128)(2,1)}, bf16[3,320,1280]{2,1,0:T(8,128)(2,1)}, u32[]{:S(2)}, u32[]{:S(2)}) collective-permute-start(bf16[3,320,1280]{2,1,0:T(8,128)(2,1)} %get-tuple-element.88), channel_id=1, source_target_pairs={{0,1},{1,0},{2,3},{3,2},{4,5},{5,4},{6,7},{7,6},{8,9},{9,8},{10,11... | collective-permute-start | bytes 7372808 | tf_op jit(solution)/shard_map/ppermute | solution.py:36
  180.6 64.2 %collective-permute-start.32 = (bf16[3,320,1280]{2,1,0:T(8,128)(2,1)}, bf16[3,320,1280]{2,1,0:T(8,128)(2,1)S(1)}, u32[]{:S(2)}, u32[]{:S(2)}) collective-permute-start(bf16[3,320,1280]{2,1,0:T(8,128)(2,1)} %add_convert_fusion), channel_id=1, source_target_pairs={{0,2},{1,3},{2,0},{3,1},{4,6},{5,7},{6,4},{7,5},{8,10},{9,11},{10,... | collective-permute-start | bytes 7372808 | tf_op jit(solution)/shard_map/ppermute | solution.py:40
  195.7 12.8 %collective-permute-start.33 = (f32[4,1280]{1,0:T(4,128)S(1)}, f32[4,1280]{1,0:T(4,128)S(1)}, u32[]{:S(2)}, u32[]{:S(2)}) collective-permute-start(f32[4,1280]{1,0:T(4,128)S(1)} %pad_maximum_fusion.3), channel_id=1, source_target_pairs={{0,1},{1,0},{2,3},{3,2},{4,5},{5,4},{6,7},{7,6},{8,9},{9,8},{10,11... | collective-permute-start | bytes 61448 | tf_op jit(solution)/shard_map/ppermute | solution.py:36
  195.9 5.2 %collective-permute-start.28 = (f32[8,6,320]{2,1,0:T(8,128)S(1)}, f32[8,6,320]{2,1,0:T(8,128)S(1)}, u32[]{:S(2)}, u32[]{:S(2)}) collective-permute-start(f32[8,6,320]{2,1,0:T(8,128)S(1)} %fusion.4), channel_id=1, source_target_pairs={{0,4},{4,0},{8,12},{12,8},{16,20},{20,16},{24,28},{28,24},{1,5},{5... | collective-permute-start | bytes 184328 | tf_op jit(solution)/shard_map/ppermute | solution.py:44
  202.3 66.3 %collective-permute-start.24 = (bf16[2,384,1280]{2,1,0:T(8,128)(2,1)}, bf16[2,384,1280]{2,1,0:T(8,128)(2,1)}, u32[]{:S(2)}, u32[]{:S(2)}) collective-permute-start(bf16[2,384,1280]{2,1,0:T(8,128)(2,1)} %get-tuple-element.83), channel_id=1, source_target_pairs={{0,1},{1,0},{2,3},{3,2},{4,5},{5,4},{6,7},{7,6},{8,9},{9,8},{10,11... | collective-permute-start | bytes 5898248 | tf_op jit(solution)/shard_map/ppermute | solution.py:36
  205.8 6.6 %collective-permute-start.30 = (f32[8,6,320]{2,1,0:T(8,128)S(1)}, f32[8,6,320]{2,1,0:T(8,128)S(1)}, u32[]{:S(2)}, u32[]{:S(2)}) collective-permute-start(f32[8,6,320]{2,1,0:T(8,128)S(1)} %add.115), channel_id=1, source_target_pairs={{0,16},{4,20},{8,24},{12,28},{16,0},{20,4},{24,8},{28,12},{1,17},{... | collective-permute-start | bytes 184328 | tf_op jit(solution)/shard_map/ppermute | solution.py:44
  208.5 28.5 %collective-permute-start.34 = (f32[4,1280]{1,0:T(4,128)S(1)}, f32[4,1280]{1,0:T(4,128)S(1)}, u32[]{:S(2)}, u32[]{:S(2)}) collective-permute-start(f32[4,1280]{1,0:T(4,128)S(1)} %fusion.16), channel_id=1, source_target_pairs={{0,2},{1,3},{2,0},{3,1},{4,6},{5,7},{6,4},{7,5},{8,10},{9,11},{10,... | collective-permute-start | bytes 61448 | tf_op jit(solution)/shard_map/ppermute | solution.py:40
  220.4 16.6 %collective-permute-start.38 = (bf16[24,1280]{1,0:T(8,128)(2,1)}, bf16[24,1280]{1,0:T(8,128)(2,1)S(1)}, u32[]{:S(2)}, u32[]{:S(2)}) collective-permute-start(bf16[24,1280]{1,0:T(8,128)(2,1)} %bitcast.84), channel_id=1, source_target_pairs={{0,4},{4,0},{8,12},{12,8},{16,20},{20,16},{24,28},{28,24},{1,5},{5... | collective-permute-start | bytes 184328 | tf_op jit(solution)/shard_map/ppermute | solution.py:44
  242.2 12.4 %collective-permute-start.40 = (bf16[24,1280]{1,0:T(8,128)(2,1)S(1)}, bf16[24,1280]{1,0:T(8,128)(2,1)S(1)}, u32[]{:S(2)}, u32[]{:S(2)}) collective-permute-start(bf16[24,1280]{1,0:T(8,128)(2,1)S(1)} %add_convert_fusion.4), channel_id=1, source_target_pairs={{0,16},{4,20},{8,24},{12,28},{16,0},{20,4},{24,8},{28,12},{1,17},{... | collective-permute-start | bytes 184328 | tf_op jit(solution)/shard_map/ppermute | solution.py:44
  258.5 9.7 %collective-permute-start.36 = (bf16[26,1280]{1,0:T(8,128)(2,1)S(1)}, bf16[26,1280]{1,0:T(8,128)(2,1)S(1)}, u32[]{:S(2)}, u32[]{:S(2)}) collective-permute-start(bf16[26,1280]{1,0:T(8,128)(2,1)S(1)} %add_convert_fusion.3), channel_id=1, source_target_pairs={{0,8},{4,12},{8,0},{12,4},{16,24},{20,28},{24,16},{28,20},{1,9},{5... | collective-permute-start | bytes 199688 | tf_op jit(solution)/shard_map/ppermute | solution.py:44
  268.3 6.3 %collective-permute-start.37 = (bf16[26,1280]{1,0:T(8,128)(2,1)S(1)}, bf16[26,1280]{1,0:T(8,128)(2,1)S(1)}, u32[]{:S(2)}, u32[]{:S(2)}) collective-permute-start(bf16[26,1280]{1,0:T(8,128)(2,1)S(1)} %add_convert_fusion.2), channel_id=1, source_target_pairs={{0,16},{4,20},{8,24},{12,28},{16,0},{20,4},{24,8},{28,12},{1,17},{... | collective-permute-start | bytes 199688 | tf_op jit(solution)/shard_map/ppermute | solution.py:44
  270.1 20.1 %collective-permute-start.25 = (bf16[384,1280]{1,0:T(8,128)(2,1)S(1)}, bf16[384,1280]{1,0:T(8,128)(2,1)S(1)}, u32[]{:S(2)}, u32[]{:S(2)}) collective-permute-start(bf16[384,1280]{1,0:T(8,128)(2,1)S(1)} %fusion.1), channel_id=1, source_target_pairs={{0,2},{1,3},{2,0},{3,1},{4,6},{5,7},{6,4},{7,5},{8,10},{9,11},{10,... | collective-permute-start | bytes 2949128 | tf_op jit(solution)/shard_map/ppermute | solution.py:40
  (41 other events, 296.6 us)
